TPU v7x, 128 devices: a whole 4x4x4 slice. The times are simulated.
128 devices in a mesh: user: 8 (over y, core), item: 16 (over x, z).
Axes of the slice: x: 4, y: 4, z: 4, core: 2. Of those that a mesh axis runs over, the one named last changes fastest.
Arguments:
- item_factor: float32 [32768, 256], P(('item', 'user')), may hold values from -36 to 36
- context_factor: float32 [4096, 256], replicated, may hold values from -6 to 6
- tile_count: int32 [8, 16], P('user', 'item'), may hold values from 16 to 128, as said below
- tile_rows: int32 [8, 16, 128], P('user', 'item'), may hold values from 0 to 63
- tile_cols: int32 [8, 16, 128], P('user', 'item'), may hold values from 0 to 31
- tile_ctx: int32 [8, 16, 128], P('user', 'item'), may hold values from 0 to 63
- nz_offsets: int32 [8, 16, 3, 128, 512], P('user', 'item'), may hold values from 0 to 63
- nz_values: float32 [8, 16, 128, 512], P('user', 'item'), may hold values from -6 to 6
Outputs:
- user_factor: float32 [32768, 256], P(('user', 'item'))
- new_items: float32 [32768, 256], P(('item', 'user'))
Inputs may be any that keep to these rules, and one draw needn't show every extreme that they name: `tile_count`: some device has all 128 tiles live; the others 128, half, a quarter or an eighth of them.
All inputs are finite; a program needn't handle non-finite values.
Results may differ from a plain program's by a relative error of at most 0.0066.
Values may be sent and summed in bfloat16 or wider, within the bound.
A program may use at most 128 MiB of HBM per device.

v0:
```python
import jax
import jax.numpy as jnp
from jax import lax
from jax.sharding import PartitionSpec as P

TILE = 64
USR_DEV = 256
ITM_DEV = 256


def solve_rows(right_side, gram):
    lower_factor = jnp.linalg.cholesky(gram)
    partway = lax.linalg.triangular_solve(
        lower_factor, right_side, left_side=False, lower=True, transpose_a=True
    )
    return lax.linalg.triangular_solve(
        lower_factor, partway, left_side=False, lower=True, transpose_a=False
    )


def mttkrp(
    live_count,
    target_ids,
    target_offsets,
    target_tiles,
    source_tiles,
    source_ids,
    source_offsets,
    context_tiles,
    context_ids,
    context_offsets,
    values,
):
    rank_width = source_tiles.shape[2]
    per_step = 8
    steps_count = (live_count + per_step - 1) // per_step
    positions = jnp.arange(TILE, dtype=jnp.int32)

    def one_hot(offsets):
        return (offsets[..., None] == positions).astype(jnp.bfloat16)

    def advance(step_index, totals):
        first = step_index * per_step
        alive = (first + jnp.arange(per_step, dtype=jnp.int32) < live_count).astype(jnp.float32)
        step_targets = lax.dynamic_slice_in_dim(target_ids, first, per_step, 0)
        step_sources = lax.dynamic_slice_in_dim(source_ids, first, per_step, 0)
        step_contexts = lax.dynamic_slice_in_dim(context_ids, first, per_step, 0)
        step_values = lax.dynamic_slice_in_dim(values, first, per_step, 0) * alive[:, None]
        source_rows = jnp.einsum(
            "bnt,btr->bnr",
            one_hot(lax.dynamic_slice_in_dim(source_offsets, first, per_step, 0)),
            source_tiles[step_sources],
            preferred_element_type=jnp.float32,
        )
        context_rows = jnp.einsum(
            "bnt,btr->bnr",
            one_hot(lax.dynamic_slice_in_dim(context_offsets, first, per_step, 0)),
            context_tiles[step_contexts],
            preferred_element_type=jnp.float32,
        )
        terms = (step_values[:, :, None] * source_rows * context_rows).astype(jnp.bfloat16)
        placed = jnp.einsum(
            "bnt,bnr->btr",
            one_hot(lax.dynamic_slice_in_dim(target_offsets, first, per_step, 0)),
            terms,
            preferred_element_type=jnp.float32,
        )
        return totals.at[step_targets].add(placed)

    totals = jnp.zeros((target_tiles, TILE, rank_width), jnp.float32)
    totals = lax.fori_loop(0, steps_count, advance, totals)
    return totals.reshape(target_tiles * TILE, rank_width)


def local(
    item_factor, context_factor, tile_count, tile_rows, tile_cols, tile_ctx, nz_offsets, nz_values
):
    highest = lax.Precision.HIGHEST
    rank_width = item_factor.shape[1]
    user_count = lax.axis_size("user")
    item_count = lax.axis_size("item")
    user_block = USR_DEV * item_count
    item_block = ITM_DEV * user_count
    users_total = user_block * user_count
    items_total = item_block * item_count
    live_count = tile_count[0, 0]
    row_ids = tile_rows[0, 0]
    col_ids = tile_cols[0, 0]
    ctx_ids = tile_ctx[0, 0]
    offsets = nz_offsets[0, 0]
    values = nz_values[0, 0]
    context_tiles = context_factor.astype(jnp.bfloat16).reshape(-1, TILE, rank_width)
    context_gram = jnp.dot(
        context_factor.T, context_factor, precision=highest, preferred_element_type=jnp.float32
    )
    item_gram = lax.psum(
        jnp.dot(item_factor.T, item_factor, precision=highest, preferred_element_type=jnp.float32),
        ("user", "item"),
    )
    item_local = lax.all_gather(item_factor.astype(jnp.bfloat16), "user", axis=0, tiled=True)
    partial_users = mttkrp(
        live_count,
        row_ids,
        offsets[0],
        user_block // TILE,
        item_local.reshape(-1, TILE, rank_width),
        col_ids,
        offsets[1],
        context_tiles,
        ctx_ids,
        offsets[2],
        values,
    )
    user_system = item_gram * context_gram
    owned_sum = lax.psum_scatter(partial_users, "item", scatter_dimension=0, tiled=True)
    raw_rows = solve_rows(owned_sum, user_system)
    raw_gram = lax.psum(
        jnp.dot(raw_rows.T, raw_rows, precision=highest, preferred_element_type=jnp.float32),
        ("user", "item"),
    )
    column_scale = jnp.sqrt(users_total / (jnp.diagonal(raw_gram) + 1e-06))
    owned_users = raw_rows * column_scale
    user_local = lax.all_gather(owned_users.astype(jnp.bfloat16), "item", axis=0, tiled=True)
    user_gram = raw_gram * column_scale[:, None] * column_scale[None, :]
    partial_items = mttkrp(
        live_count,
        col_ids,
        offsets[1],
        item_block // TILE,
        user_local.reshape(-1, TILE, rank_width),
        row_ids,
        offsets[0],
        context_tiles,
        ctx_ids,
        offsets[2],
        values,
    )
    owned_items = lax.psum_scatter(partial_items, "user", scatter_dimension=0, tiled=True)
    item_raw = solve_rows(owned_items, user_gram * context_gram)
    item_squares = lax.psum(jnp.sum(item_raw * item_raw, axis=0), ("user", "item"))
    new_items = item_raw * jnp.sqrt(items_total / (item_squares + 1e-06))
    return (owned_users, new_items)


def solution(mesh):
    in_specs = (
        P(("item", "user"), None),
        P(),
        P("user", "item"),
        P("user", "item", None),
        P("user", "item", None),
        P("user", "item", None),
        P("user", "item", None, None, None),
        P("user", "item", None, None),
    )
    out_specs = (P(("user", "item"), None), P(("item", "user"), None))
    return jax.shard_map(local, mesh=mesh, in_specs=in_specs, out_specs=out_specs, check_vma=False)
```

profile of v0, /device:TPU:1, one launch (start us, length us, event | category | flops | bytes accessed | tf_op | source)
XLA Modules:
  0.0 921.2 jit_solution(2475890599702103652)
XLA Ops:
  17.2 20.4 %all-gather.3.cloned.1.call-done = bf16[2048,256]{1,0:T(8,128)(2,1)} async-done(((bf16[256,256]{1,0:T(8,128)(2,1)}), bf16[2048,256]{1,0:T(8,128)(2,1)}) %all-gather.3.cloned.1.call-update) | async-done | bytes 1048592 | tf_op jit(solution)/shard_map/all_gather | solution.py:100
  40.1 28.9 %while.32 = (s32[]{:T(128)}, f32[64,64,256]{2,1,0:T(8,128)}, s32[]{:T(128)}, s32[128]{0:T(128)S(1)}, s32[128,512]{1,0:T(8,128)}, /*index=5*/f32[128,512]{1,0:T(8...) while((s32[]{:T(128)}, f32[64,64,256]{2,1,0:T(8,128)}, ...), condition=%wide.region_7.9_spmd.clone.clone, body=%wide.region_5.8_spmd.clone.clone.sunk | while | flops 406722656 | bytes 12264079 | solution.py:71
  48.3 3.6 fusion.83
  62.7 3.6 fusion.83
  69.7 90.2 %all-reduce.4.cloned.1.call-done = f32[256,256]{0,1:T(8,128)} async-done(((f32[256,256]{0,1:T(8,128)}), f32[256,256]{0,1:T(8,128)}) %all-reduce.4.cloned.1.call-update) | async-done | bytes 262160 | tf_op jit(solution)/shard_map/psum | solution.py:96
  159.9 10.2 %fusion.46 = (f32[256,256]{0,1:T(8,128)S(1)}, f32[256,256]{0,1:T(8,128)S(1)}) fusion(f32[256,256]{0,1:T(8,128)} %all-reduce.4.cloned.1.call-done, f32[4096,256]{1,0:T(8,128)} %param.18), kind=kOutput, calls=%fused_computation.122 | convolution fusion | flops 3221291008 | bytes 4980736 | tf_op jit(solution)/shard_map/dot_general | solution.py:93
  170.3 11.7 %cholesky.130 = f32[128,128]{1,0:T(8,128)S(1)} custom-call(f32[128,128]{1,0:T(8,128)S(1)} %cholesky.194), custom_call_target="Cholesky" | custom-call | tf_op jit(solution)/shard_map/jit(cholesky)/cholesky | solution.py:12
  182.1 9.9 %custom-call.19 = f32[1,128,128]{1,2,0:T(8,128)S(1)} custom-call(f32[1,128,128]{2,1,0:T(8,128)S(1)} %get-tuple-element.432), custom_call_target="InvertDiagBlocksLowerTriangular" | custom-call | tf_op jit(solution)/shard_map/jit(cholesky)/cholesky | solution.py:12
  192.5 11.7 %cholesky.147 = f32[128,128]{1,0:T(8,128)S(1)} custom-call(f32[128,128]{1,0:T(8,128)S(1)} %convolution_subtract_fusion.5), custom_call_target="Cholesky" | custom-call | tf_op jit(solution)/shard_map/jit(cholesky)/cholesky | solution.py:12
  206.3 3.9 while.34
  210.2 19.7 %custom-call.20 = f32[2,128,128]{1,2,0:T(8,128)S(1)} custom-call(f32[2,128,128]{2,1,0:T(8,128)S(1)} %get-tuple-element.319), custom_call_target="InvertDiagBlocksLowerTriangular" | custom-call | tf_op jit(solution)/shard_map/triangular_solve/custom-call.0 | solution.py:13
  229.9 116.3 %reduce-scatter.3.cloned.1.call-done = f32[256,256]{1,0:T(8,128)} async-done(((f32[4096,256]{1,0:T(8,128)}), f32[256,256]{1,0:T(8,128)}) %reduce-scatter.3.cloned.1.call-update) | async-done | bytes 262160 | tf_op jit(solution)/shard_map/reduce_scatter | solution.py:115
  351.1 142.3 %all-reduce.6.cloned.1.call-done = f32[256,256]{0,1:T(8,128)} async-done(((f32[256,256]{0,1:T(8,128)}), f32[256,256]{0,1:T(8,128)}) %all-reduce.6.cloned.1.call-update) | async-done | bytes 262160 | tf_op jit(solution)/shard_map/psum | solution.py:117
  497.9 44.1 %all-gather.5.cloned.1.call-done = bf16[4096,256]{0,1:T(8,128)(2,1)} async-done(((bf16[256,256]{0,1:T(8,128)(2,1)}), bf16[4096,256]{0,1:T(8,128)(2,1)}) %all-gather.5.cloned.1.call-update) | async-done | bytes 2097168 | tf_op jit(solution)/shard_map/all_gather | solution.py:123
  542.0 4.1 copy.25
  546.3 29.7 %while.33 = (s32[]{:T(128)}, f32[32,64,256]{2,1,0:T(8,128)S(1)}, s32[]{:T(128)}, s32[128]{0:T(128)S(1)}, s32[128,512]{1,0:T(8,128)}, /*index=5*/f32[128,512]{1,0...) while((s32[]{:T(128)}, f32[32,64,256]{2,1,0:T(8,128)S(1)}, ...), condition=%wide.region_12.16_spmd.clone.clone, body=%wide.region_10.0_spmd.clone.clone.sunk | while | flops 406722656 | bytes 12264079 | solution.py:71
  571.4 3.6 fusion.87
  578.4 11.7 %cholesky.164 = f32[128,128]{1,0:T(8,128)S(1)} custom-call(f32[128,128]{1,0:T(8,128)S(1)} %cholesky.197), custom_call_target="Cholesky" | custom-call | tf_op jit(solution)/shard_map/jit(cholesky)/cholesky | solution.py:12
  590.2 9.8 %custom-call.22 = f32[1,128,128]{1,2,0:T(8,128)S(1)} custom-call(f32[1,128,128]{2,1,0:T(8,128)S(1)} %get-tuple-element.428), custom_call_target="InvertDiagBlocksLowerTriangular" | custom-call | tf_op jit(solution)/shard_map/jit(cholesky)/cholesky | solution.py:12
  600.5 11.7 %cholesky.181 = f32[128,128]{1,0:T(8,128)S(1)} custom-call(f32[128,128]{1,0:T(8,128)S(1)} %convolution_subtract_fusion.4), custom_call_target="Cholesky" | custom-call | tf_op jit(solution)/shard_map/jit(cholesky)/cholesky | solution.py:12
  614.8 4.1 while.35
  618.9 19.7 %custom-call.23 = f32[2,128,128]{1,2,0:T(8,128)S(1)} custom-call(f32[2,128,128]{2,1,0:T(8,128)S(1)} %get-tuple-element.321), custom_call_target="InvertDiagBlocksLowerTriangular" | custom-call | tf_op jit(solution)/shard_map/triangular_solve/custom-call.0 | solution.py:13
  638.6 175.7 %reduce-scatter.5.cloned.1.call-done = f32[256,256]{1,0:T(8,128)} async-done(((f32[2048,256]{1,0:T(8,128)}), f32[256,256]{1,0:T(8,128)}) %reduce-scatter.5.cloned.1.call-update) | async-done | bytes 262160 | tf_op jit(solution)/shard_map/reduce_scatter | solution.py:138
  818.1 94.8 %psum.23 = f32[256]{0:T(256)S(1)} all-reduce(f32[256]{0:T(256)S(1)} %multiply_reduce_fusion), channel_id=1, replica_groups=mesh['user'=8,'item'=16] {'user','item'}, use_global_device_ids=true, to_apply=%region_15.19 | all-reduce | flops 256 | bytes 2048 | tf_op jit(solution)/shard_map/psum | solution.py:140
  (140 shorter events, 86.8 us)
Async XLA Ops:
  8.0 29.6 %all-gather.3.cloned.1.call-start = ((), (), s32[]{:S(2)}) async-start(), calls=%async_computation.3 | async-start | bytes 1179648 | tf_op jit(solution)/shard_map/all_gather | solution.py:100
  9.7 150.2 %all-reduce.4.cloned.1.call-start = ((), (), s32[]{:S(2)}) async-start(), calls=%async_computation.2 | async-start | bytes 524288 | tf_op jit(solution)/shard_map/psum | solution.py:96
  12.1 334.1 %reduce-scatter.3.cloned.1.call-start = ((), (), s32[]{:S(2)}) async-start(), calls=%async_computation.4 | async-start | bytes 4456448 | tf_op jit(solution)/shard_map/reduce_scatter | solution.py:115
  14.8 25.3 %copy-start.4 = (s32[1,1,128]{2,1,0:T(1,128)S(1)}, s32[1,1,128]{2,1,0:T(1,128)}, u32[]{:S(2)}) copy-start(s32[1,1,128]{2,1,0:T(1,128)} %param.22) | copy-start | bytes 1540
  14.8 25.3 %copy-start.5 = (s32[1,1,128]{2,1,0:T(1,128)S(1)}, s32[1,1,128]{2,1,0:T(1,128)}, u32[]{:S(2)}) copy-start(s32[1,1,128]{2,1,0:T(1,128)} %param.20) | copy-start | bytes 1540
  14.8 25.3 %copy-start.6 = (s32[1,1,128]{2,1,0:T(1,128)S(1)}, s32[1,1,128]{2,1,0:T(1,128)}, u32[]{:S(2)}) copy-start(s32[1,1,128]{2,1,0:T(1,128)} %param.21) | copy-start | bytes 1540
  69.0 0.7 copy-start.3
  69.0 101.1 %copy-start.1 = (bf16[64,64,256]{2,1,0:T(8,128)(2,1)}, bf16[64,64,256]{2,1,0:T(8,128)(2,1)S(1)}, u32[]{:S(2)}) copy-start(bf16[64,64,256]{2,1,0:T(8,128)(2,1)S(1)} %get-tuple-element.818) | copy-start | bytes 6291460
  69.0 424.4 %all-reduce.6.cloned.1.call-start = ((), (), s32[]{:S(2)}) async-start(), calls=%async_computation.5 | async-start | bytes 524288 | tf_op jit(solution)/shard_map/psum | solution.py:117
  351.0 191.0 %all-gather.5.cloned.1.call-start = ((), (), s32[]{:S(2)}) async-start(), calls=%async_computation.6 | async-start | bytes 2228224 | tf_op jit(solution)/shard_map/all_gather | solution.py:123
  497.8 316.4 %reduce-scatter.5.cloned.1.call-start = ((), (), s32[]{:S(2)}) async-start(), calls=%async_computation.7 | async-start | bytes 2359296 | tf_op jit(solution)/shard_map/reduce_scatter | solution.py:138
  546.3 31.1 %copy-start.2 = (f32[256,256]{0,1:T(8,128)S(1)}, f32[256,256]{0,1:T(8,128)}, u32[]{:S(2)}) copy-start(f32[256,256]{0,1:T(8,128)} %get-tuple-element.409) | copy-start | bytes 786436
  576.0 1.4 copy-start
Sparse Core Ops, SparseCore 0:
  10.5 27.0 all-gather.2
  69.1 277.0 reduce-scatter.2
  498.0 43.9 all-gather.4
  577.5 236.7 reduce-scatter.4
Sparse Core Ops, SparseCore 1:
  14.9 144.9 all-reduce.3
  351.1 142.2 all-reduce.5
where the time goes:
time: 936 us; the launch traced here: 921 us
  waiting for transfers between devices  589 us (63%)
  other arithmetic  128 us (14%)
  blocking collectives  94.8 us (10%)
  matrix products  47.1 us (5%)
  local copies, waits for them, and re-layouts  41.6 us (4%)
  between operations  18.9 us (2%)
    reduce_scatter x1, waiting for transfers between devices, local(): lax.psum_scatter(partial_items, 'user', scatter_dimension=0, tiled=True)  176 us
    psum x1, waiting for transfers between devices, local(): lax.psum(jnp.dot(raw_rows.T, raw_rows, precision=highest, preferred_eleme...  142 us
    reduce_scatter x1, waiting for transfers between devices, local(): lax.psum_scatter(partial_users, 'item', scatter_dimension=0, tiled=True)  116 us
    psum x1, blocking collectives, local(): lax.psum(jnp.sum(item_raw * item_raw, axis=0), ('user', 'item'))  94.8 us
    psum x1, waiting for transfers between devices, local(): lax.psum(jnp.dot(item_factor.T, item_factor, precision=highest, preferred...  90.2 us
    another operation x13, other arithmetic, solve_rows(): lower_factor = jnp.linalg.cholesky(gram)  68.7 us
    all_gather x1, waiting for transfers between devices, local(): lax.all_gather(owned_users.astype(jnp.bfloat16), 'item', axis=0, tiled=True)  44.1 us
    another operation x5, other arithmetic, solve_rows(): lax.linalg.triangular_solve(lower_factor, right_side, left_side=False, lo...  39.4 us
  transfers between devices with their start and end apart: 6, of which 6 were waited for; matrix products, arithmetic and copies ran while one was open for 18% of the time, Pallas kernels for 0%

commit v1 on v0

v1 whole, which is shorter than its diff:
```python
import functools

import jax
import jax.numpy as jnp
from jax import lax
from jax.experimental import pallas as pl
from jax.experimental.pallas import tpu as pltpu
from jax.sharding import PartitionSpec as P

TILE = 64
UNROLL = 16
BLOCK = 32
HIGHEST = lax.Precision.HIGHEST
MESH = pl.DeviceIdType.MESH
VMEM_SPEC = pl.BlockSpec(memory_space=pltpu.VMEM)
SMEM_SPEC = pl.BlockSpec(memory_space=pltpu.SMEM)


def dot(left, right):
    return jnp.dot(left, right, precision=HIGHEST, preferred_element_type=jnp.float32)


def dot_rows(left, right):
    return lax.dot_general(
        left, right, (((0,), (0,)), ((), ())), precision=HIGHEST, preferred_element_type=jnp.float32
    )


def mttkrp_kernel(
    count,
    target_ids,
    source_ids,
    context_ids,
    target_offsets,
    source_offsets,
    context_offsets,
    values,
    source,
    context,
    out,
    totals,
):
    totals[...] = jnp.zeros_like(totals)
    positions = lax.broadcasted_iota(jnp.int32, (TILE, target_offsets.shape[1]), 0)

    def one_hot(row):
        return jnp.where(positions == row, 1.0, 0.0).astype(jnp.bfloat16)

    def gather(tile, row):
        return lax.dot_general(
            tile, one_hot(row), (((0,), (0,)), ((), ())), preferred_element_type=jnp.float32
        )

    def group(step, carry):
        first = pl.multiple_of(step * UNROLL, UNROLL)
        targets = target_offsets[pl.ds(first, UNROLL), :]
        sources = source_offsets[pl.ds(first, UNROLL), :]
        contexts = context_offsets[pl.ds(first, UNROLL), :]
        weights = values[pl.ds(first, UNROLL), :]
        for at in range(UNROLL):
            row = slice(at, at + 1)
            source_rows = gather(source[source_ids[first + at]], sources[row])
            context_rows = gather(context[context_ids[first + at]], contexts[row])
            terms = (weights[row] * source_rows * context_rows).astype(jnp.bfloat16)
            totals[target_ids[first + at]] += lax.dot_general(
                one_hot(targets[row]),
                terms,
                (((1,), (1,)), ((), ())),
                preferred_element_type=jnp.float32,
            )
        return carry

    lax.fori_loop(0, count[0] // UNROLL, group, 0)
    out[...] = totals[...].astype(out.dtype)


def mttkrp(count, target, source, context, values, source_tiles, context_tiles, tiles):
    shape = (tiles, TILE, source_tiles.shape[2])
    return pl.pallas_call(
        mttkrp_kernel,
        out_shape=jax.ShapeDtypeStruct(shape, jnp.bfloat16),
        in_specs=[SMEM_SPEC] * 4 + [VMEM_SPEC] * 6,
        out_specs=VMEM_SPEC,
        scratch_shapes=[pltpu.VMEM(shape, jnp.float32)],
        compiler_params=pltpu.CompilerParams(vmem_limit_bytes=48 * 2**20),
        name="mttkrp",
    )(
        count,
        target[0],
        source[0],
        context[0],
        target[1],
        source[1],
        context[1],
        values,
        source_tiles,
        context_tiles,
    )


def greet(groups):
    barrier = pltpu.get_barrier_semaphore()
    total = 0
    for axis, size in groups:
        me = lax.axis_index(axis)
        for ahead in range(1, size):
            pl.semaphore_signal(
                barrier, inc=1, device_id={axis: lax.rem(me + ahead, size)}, device_id_type=MESH
            )
        total += size - 1
    pl.semaphore_wait(barrier, total)


def send_all(axis, size, source, target, sems):
    me = lax.axis_index(axis)
    copies = []
    for ahead in range(1, size):
        peer = lax.rem(me + ahead, size)
        copy = pltpu.make_async_remote_copy(
            src_ref=source(peer, ahead),
            dst_ref=target(me, ahead),
            send_sem=sems.at[0, ahead - 1],
            recv_sem=sems.at[1, ahead - 1],
            device_id={axis: peer},
            device_id_type=MESH,
        )
        copy.start()
        copies.append(copy)
    return copies


def all_reduce(gram, scattered, summed, sems, result, axis_sizes):
    users, items = axis_sizes
    rows = gram.shape[0] // items
    user, item = lax.axis_index("user"), lax.axis_index("item")
    first = send_all(
        "item",
        items,
        lambda peer, ahead: gram.at[pl.ds(pl.multiple_of(peer * rows, rows), rows)],
        lambda me, ahead: scattered.at[me],
        sems.at[0],
    )
    scattered[item] = gram[pl.ds(pl.multiple_of(item * rows, rows), rows), :]
    for copy in first:
        copy.wait_recv()
    summed[user] = jnp.sum(scattered[...], axis=0)
    second = send_all(
        "user",
        users,
        lambda peer, ahead: summed.at[user],
        lambda me, ahead: summed.at[me],
        sems.at[1],
    )
    for copy in second:
        copy.wait_recv()
    own = pl.ds(pl.multiple_of(item * rows, rows), rows)
    result[own, :] = jnp.sum(summed[...], axis=0)
    third = send_all(
        "item",
        items,
        lambda peer, ahead: result.at[own],
        lambda me, ahead: result.at[own],
        sems.at[2],
    )
    for copy in third:
        copy.wait_recv()
    for copy in first + second + third:
        copy.wait_send()


def reduce_scratch(axis_sizes, width):
    users, items = axis_sizes
    rows = width // items
    return [
        pltpu.VMEM((width, width), jnp.float32),
        pltpu.VMEM((items, rows, width), jnp.float32),
        pltpu.VMEM((users, rows, width), jnp.float32),
        pltpu.SemaphoreType.DMA((3, 2, items - 1)),
    ]


def invert(work):
    width = work.shape[0]
    down = lax.broadcasted_iota(jnp.int32, (BLOCK, BLOCK), 0)
    across = lax.broadcasted_iota(jnp.int32, (BLOCK, BLOCK), 1)
    lanes = lax.broadcasted_iota(jnp.int32, (BLOCK, width), 1) // BLOCK
    rows = lax.broadcasted_iota(jnp.int32, (width, BLOCK), 0) // BLOCK
    full_lanes = lax.broadcasted_iota(jnp.int32, (width, width), 1) // BLOCK
    for block in range(width // BLOCK):
        span = slice(block * BLOCK, (block + 1) * BLOCK)
        pivot = work[span, span]
        for at in range(BLOCK):
            inverse = 1.0 / pivot[at : at + 1, at : at + 1]
            row = jnp.where(across[:1] == at, inverse, pivot[at : at + 1, :] * inverse)
            column = pivot[:, at : at + 1]
            kept = jnp.where(across == at, 0.0, pivot)
            pivot = jnp.where(down == at, row, kept - column * row)
        panel = dot(pivot, work[span, :])
        panel = jnp.where(lanes == block, jnp.concatenate([pivot] * (width // BLOCK), axis=1), panel)
        column = jnp.where(rows == block, 0.0, work[:, span])
        kept = jnp.where(full_lanes == block, 0.0, work[...])
        work[...] = kept - dot(column, panel)
        work[span, :] = panel


def gather_kernel(
    axis_sizes, item_factor, context_factor, items, context, system, context_gram, gram, scattered,
    summed, gram_sems, sems
):
    users = axis_sizes[0]
    user = lax.axis_index("user")
    items[user] = item_factor[...].astype(jnp.bfloat16)
    greet((("user", axis_sizes[0]), ("item", axis_sizes[1])))
    copies = send_all(
        "user", users, lambda peer, ahead: items.at[user], lambda me, ahead: items.at[me], sems
    )
    gram[...] = dot_rows(item_factor[...], item_factor[...])
    step_rows = 512
    context_gram[...] = jnp.zeros_like(context_gram)

    def step(index, carry):
        span = pl.ds(pl.multiple_of(index * step_rows, step_rows), step_rows)
        chunk = context_factor[span, :]
        context[span, :] = chunk.astype(jnp.bfloat16)
        context_gram[...] += dot_rows(chunk, chunk)
        return carry

    lax.fori_loop(0, context_factor.shape[0] // step_rows, step, 0)
    all_reduce(gram, scattered, summed, gram_sems, system, axis_sizes)
    system[...] = system[...] * context_gram[...]
    for copy in copies:
        copy.wait_recv()
    for copy in copies:
        copy.wait_send()


def gather_items(item_factor, context_factor, axis_sizes):
    users, items = axis_sizes
    rows, width = item_factor.shape
    square = jax.ShapeDtypeStruct((width, width), jnp.float32)
    return pl.pallas_call(
        functools.partial(gather_kernel, axis_sizes),
        out_shape=(
            jax.ShapeDtypeStruct((users, rows, width), jnp.bfloat16),
            jax.ShapeDtypeStruct(context_factor.shape, jnp.bfloat16),
            square,
            square,
        ),
        in_specs=[VMEM_SPEC] * 2,
        out_specs=(VMEM_SPEC,) * 4,
        scratch_shapes=reduce_scratch(axis_sizes, width)
        + [pltpu.SemaphoreType.DMA((2, users - 1))],
        compiler_params=pltpu.CompilerParams(
            collective_id=0, has_side_effects=True, vmem_limit_bytes=32 * 2**20
        ),
        name="gather_items",
    )(item_factor, context_factor)


def user_kernel(
    axis_sizes, partial, system, raw, gathered, raw_gram, arrived, work, gram, scattered, summed,
    gram_sems, sems
):
    items = axis_sizes[1]
    item = lax.axis_index("item")
    greet((("user", axis_sizes[0]), ("item", axis_sizes[1])))
    copies = send_all(
        "item",
        items,
        lambda peer, ahead: partial.at[peer],
        lambda me, ahead: arrived.at[ahead - 1],
        sems.at[0],
    )
    work[...] = system[...]
    invert(work)
    total = partial[item].astype(jnp.float32)
    for ahead in range(1, items):
        copies[ahead - 1].wait_recv()
        total = total + arrived[ahead - 1].astype(jnp.float32)
    raw[...] = dot(total, work[...])
    gathered[item] = raw[...].astype(jnp.bfloat16)
    spread = send_all(
        "item", items, lambda peer, ahead: gathered.at[item], lambda me, ahead: gathered.at[me], sems.at[1]
    )
    gram[...] = dot_rows(raw[...], raw[...])
    all_reduce(gram, scattered, summed, gram_sems, raw_gram, axis_sizes)
    for copy in spread:
        copy.wait_recv()
    for copy in copies + spread:
        copy.wait_send()


def update_users(partial, system, axis_sizes):
    users, items = axis_sizes
    _, rows, width = partial.shape
    square = jax.ShapeDtypeStruct((width, width), jnp.float32)
    return pl.pallas_call(
        functools.partial(user_kernel, axis_sizes),
        out_shape=(
            jax.ShapeDtypeStruct((rows, width), jnp.float32),
            jax.ShapeDtypeStruct(partial.shape, jnp.bfloat16),
            square,
        ),
        in_specs=[VMEM_SPEC] * 2,
        out_specs=(VMEM_SPEC,) * 3,
        scratch_shapes=[
            pltpu.VMEM((items - 1, rows, width), jnp.bfloat16),
            pltpu.VMEM((width, width), jnp.float32),
        ]
        + reduce_scratch(axis_sizes, width)
        + [pltpu.SemaphoreType.DMA((2, 2, items - 1))],
        compiler_params=pltpu.CompilerParams(
            collective_id=1, has_side_effects=True, vmem_limit_bytes=32 * 2**20
        ),
        name="update_users",
    )(partial, system)


def item_kernel(
    axis_sizes, partial, raw_gram, context_gram, raw, new_items, user_factor, arrived, work,
    user_sums, item_sums, user_sems, item_sems, sems
):
    users, items = axis_sizes
    user, item = lax.axis_index("user"), lax.axis_index("item")
    greet((("user", users), ("item", items)))
    copies = send_all(
        "user",
        users,
        lambda peer, ahead: partial.at[peer],
        lambda me, ahead: arrived.at[ahead - 1],
        sems,
    )
    width = work.shape[0]
    rows_total = jnp.float32(user_factor.shape[0] * users * items)
    down = lax.broadcasted_iota(jnp.int32, (width, width), 0)
    across = lax.broadcasted_iota(jnp.int32, (width, width), 1)
    diagonal = jnp.where(down == across, raw_gram[...], 0.0)
    scale_row = jnp.sqrt(rows_total / (jnp.sum(diagonal, axis=0, keepdims=True) + 1e-06))
    scale_column = jnp.sqrt(rows_total / (jnp.sum(diagonal, axis=1, keepdims=True) + 1e-06))
    user_factor[...] = raw[...] * scale_row
    work[...] = raw_gram[...] * scale_column * scale_row * context_gram[...]
    invert(work)
    total = partial[user].astype(jnp.float32)
    for ahead in range(1, users):
        copies[ahead - 1].wait_recv()
        total = total + arrived[ahead - 1].astype(jnp.float32)
    item_raw = dot(total * scale_row, work[...])
    squares = jnp.sum(item_raw * item_raw, axis=0, keepdims=True)
    user_sums[user] = jnp.broadcast_to(squares, user_sums.shape[1:])
    first = send_all(
        "user", users, lambda peer, ahead: user_sums.at[user], lambda me, ahead: user_sums.at[me], user_sems
    )
    for copy in first:
        copy.wait_recv()
    item_sums[item] = jnp.sum(user_sums[...], axis=0)
    second = send_all(
        "item", items, lambda peer, ahead: item_sums.at[item], lambda me, ahead: item_sums.at[me], item_sems
    )
    for copy in second:
        copy.wait_recv()
    squares = jnp.sum(item_sums[...], axis=0)[:1]
    new_items[...] = item_raw * jnp.sqrt(rows_total / (squares + 1e-06))
    for copy in copies + first + second:
        copy.wait_send()


def update_items(partial, raw_gram, context_gram, raw, axis_sizes):
    users, items = axis_sizes
    _, rows, width = partial.shape
    out = jax.ShapeDtypeStruct((rows, width), jnp.float32)
    return pl.pallas_call(
        functools.partial(item_kernel, axis_sizes),
        out_shape=(out, out),
        in_specs=[VMEM_SPEC] * 4,
        out_specs=(VMEM_SPEC,) * 2,
        scratch_shapes=[
            pltpu.VMEM((users - 1, rows, width), jnp.bfloat16),
            pltpu.VMEM((width, width), jnp.float32),
            pltpu.VMEM((users, 8, width), jnp.float32),
            pltpu.VMEM((items, 8, width), jnp.float32),
            pltpu.SemaphoreType.DMA((2, users - 1)),
            pltpu.SemaphoreType.DMA((2, items - 1)),
            pltpu.SemaphoreType.DMA((2, users - 1)),
        ],
        compiler_params=pltpu.CompilerParams(
            collective_id=2, has_side_effects=True, vmem_limit_bytes=32 * 2**20
        ),
        name="update_items",
    )(partial, raw_gram, context_gram, raw)


def local(
    item_factor, context_factor, tile_count, tile_rows, tile_cols, tile_ctx, nz_offsets, nz_values
):
    axis_sizes = (lax.axis_size("user"), lax.axis_size("item"))
    users, items = axis_sizes
    rows, width = item_factor.shape
    count = tile_count.reshape(1)
    offsets = nz_offsets[0, 0]
    values = nz_values[0, 0]
    user_side = (tile_rows[0, 0], offsets[0])
    item_side = (tile_cols[0, 0], offsets[1])
    context_side = (tile_ctx[0, 0], offsets[2])
    item_rows, context, system, context_gram = gather_items(item_factor, context_factor, axis_sizes)
    context_tiles = context.reshape(-1, TILE, width)
    partial_users = mttkrp(
        count, user_side, item_side, context_side, values,
        item_rows.reshape(-1, TILE, width), context_tiles, items * rows // TILE,
    )
    raw, user_rows, raw_gram = update_users(
        partial_users.reshape(items, rows, width), system, axis_sizes
    )
    partial_items = mttkrp(
        count, item_side, user_side, context_side, values,
        user_rows.reshape(-1, TILE, width), context_tiles, users * rows // TILE,
    )
    new_items, user_factor = update_items(
        partial_items.reshape(users, rows, width), raw_gram, context_gram, raw, axis_sizes
    )
    return (user_factor, new_items)


def solution(mesh):
    in_specs = (
        P(("item", "user"), None),
        P(),
        P("user", "item"),
        P("user", "item", None),
        P("user", "item", None),
        P("user", "item", None),
        P("user", "item", None, None, None),
        P("user", "item", None, None),
    )
    out_specs = (P(("user", "item"), None), P(("item", "user"), None))
    return jax.shard_map(local, mesh=mesh, in_specs=in_specs, out_specs=out_specs, check_vma=False)
```

time: 936 us -> 250 us (0.27); the launches traced: 921 us -> 249 us
  waiting for transfers between devices: 589 us -> 0 us
  Pallas kernels: 0 us -> 241 us
  other arithmetic: 128 us -> 0 us
  blocking collectives: 94.8 us -> 0 us
  matrix products: 47.1 us -> 0 us
  local copies, waits for them, and re-layouts: 41.6 us -> 7.04 us
  between operations: 18.9 us -> 1.35 us
    reduce_scatter x2 -> x0, waiting for transfers between devices: 292 us -> none  [the longest x1 176 us: local(): lax.psum_scatter(partial_items, 'user', scatter_dimension=0, tiled=True)]
    pallas_call x0 -> x5, Pallas kernels: none -> 241 us  [the longest x1 88.1 us: update_users(): pl.pallas_call(functools.partial(user_kernel, axis_sizes), out_shape=(jax...]
    psum x2 -> x0, waiting for transfers between devices: 232 us -> none  [the longest x1 142 us: local(): lax.psum(jnp.dot(raw_rows.T, raw_rows, precision=highest, preferred_eleme...]
    another operation x18 -> x0, other arithmetic: 108 us -> none  [the longest x13 68.7 us: solve_rows(): lower_factor = jnp.linalg.cholesky(gram)]
    psum x1 -> x0, blocking collectives: 94.8 us -> none  [local(): lax.psum(jnp.sum(item_raw * item_raw, axis=0), ('user', 'item'))]
    all_gather x2 -> x0, waiting for transfers between devices: 64.5 us -> none  [the longest x1 44.1 us: local(): lax.all_gather(owned_users.astype(jnp.bfloat16), 'item', axis=0, tiled=True)]
    dot_general x11 -> x0, matrix products: 38.8 us -> none  [the longest x4 14.3 us: advance(): jnp.einsum('bnt,bnr->btr', one_hot(lax.dynamic_slice_in_dim(target_offset...]
    gather x9 -> x0, local copies, waits for them, and re-layouts: 15.9 us -> none  [the longest x4 7.89 us: advance(): source_tiles[step_sources]]
  transfers between devices with their start and end apart: 6 -> 0, of which waited for: 6 -> 0; matrix products, arithmetic and copies ran while one was open for 18% -> 0% of each run, Pallas kernels for 0% -> 0%
where the time goes in v1:
time: 250 us; the launch traced here: 249 us
  Pallas kernels  241 us (96%)
  local copies, waits for them, and re-layouts  7.04 us (3%)
    pallas_call x1, Pallas kernels, update_users(): pl.pallas_call(functools.partial(user_kernel, axis_sizes), out_shape=(jax...  88.1 us
    pallas_call x2, Pallas kernels, mttkrp(): pl.pallas_call(mttkrp_kernel, out_shape=jax.ShapeDtypeStruct(shape, jnp.b...  78.1 us
    pallas_call x1, Pallas kernels, update_items(): pl.pallas_call(functools.partial(item_kernel, axis_sizes), out_shape=(out...  43.3 us
    pallas_call x1, Pallas kernels, gather_items(): pl.pallas_call(functools.partial(gather_kernel, axis_sizes), out_shape=(j...  31.6 us
    unnamed x16, local copies, waits for them, and re-layouts  5.88 us

profile of v1, /device:TPU:1, one launch (start us, length us, event | category | flops | bytes accessed | tf_op | source)
XLA Modules:
  0.0 249.5 jit_solution(17973204227900161094)
XLA Ops:
  1.3 1.2 slice_bitcast_fusion
  2.4 0.0 copy-start.1
  2.5 2.2 copy-done.1
  4.6 0.0 copy-start.3
  4.6 0.9 copy-done.3
  5.6 0.0 copy-start.2
  5.6 0.0 copy-start.4
  5.6 0.0 copy-start.5
  5.6 0.0 copy-start.6
  5.6 31.6 %gather_items.1 = (bf16[8,256,256]{2,1,0:T(8,128)(2,1)S(1)}, bf16[4096,256]{1,0:T(8,128)(2,1)S(1)}, f32[256,256]{1,0:T(8,128)S(1)}, f32[256,256]{1,0:T(8,128)S(1)}) custom-call(f32[256,256]{1,0:T(8,128)S(1)} %copy-done.3, f32[4096,256]{1,0:T(8,128)S(1)} %copy-done.1), custom_call_target="tpu_custom_call" | custom-call | tf_op jit(solution)/shard_map/gather_items/pallas_call | solution.py:241
  37.2 0.0 copy-start
  37.2 1.3 copy-done
  38.5 0.0 copy-done.2
  38.5 0.0 copy-done.4
  38.6 0.0 copy-done.5
  38.6 0.0 copy-done.6
  38.6 39.1 %mttkrp.2 = bf16[64,64,256]{2,1,0:T(8,128)(2,1)S(1)} custom-call(s32[1]{0:T(128)} %bitcast.16.count, s32[128]{0:T(128)S(1)} %bitcast.28, s32[128]{0:T(128)S(1)} %bitcast.26, s32[128]{0:T(128)S(1)} %bitcast.30, s32[128,512]{1,0:T(8,128)S(1)} %get-tuple-element.22.target_offsets.source_offsets, s32[128,512]{1,0:T(8,128)S(1)} %get-tuple-element.21.source_offsets.target_offsets, ...), custom_call_target="tpu_custom_call" | custom-call | tf_op jit(solution)/shard_map/mttkrp/pallas_call | solution.py:79
  77.7 88.1 %update_users.1 = (f32[256,256]{1,0:T(8,128)S(1)}, bf16[16,256,256]{2,1,0:T(8,128)(2,1)S(1)}, f32[256,256]{1,0:T(8,128)S(1)}) custom-call(bf16[16,256,256]{2,1,0:T(8,128)(2,1)S(1)} %bitcast.20, f32[256,256]{1,0:T(8,128)S(1)} %get-tuple-element.13.system), custom_call_target="tpu_custom_call" | custom-call | tf_op jit(solution)/shard_map/update_users/pallas_call | solution.py:297
  165.8 38.9 %mttkrp.3 = bf16[32,64,256]{2,1,0:T(8,128)(2,1)S(1)} custom-call(s32[1]{0:T(128)} %bitcast.17.count, s32[128]{0:T(128)S(1)} %bitcast.27, s32[128]{0:T(128)S(1)} %bitcast.29, s32[128]{0:T(128)S(1)} %bitcast.31, s32[128,512]{1,0:T(8,128)S(1)} %get-tuple-element.21.source_offsets.target_offsets, s32[128,512]{1,0:T(8,128)S(1)} %get-tuple-element.22.target_offsets.source_offsets, ...), custom_call_target="tpu_custom_call" | custom-call | tf_op jit(solution)/shard_map/mttkrp/pallas_call | solution.py:79
  204.7 43.3 %update_items.1 = (f32[256,256]{1,0:T(8,128)S(1)}, f32[256,256]{1,0:T(8,128)S(1)}) custom-call(bf16[8,256,256]{2,1,0:T(8,128)(2,1)S(1)} %bitcast.21, f32[256,256]{1,0:T(8,128)S(1)} %get-tuple-element.15.raw_gram, f32[256,256]{1,0:T(8,128)S(1)} %get-tuple-element.16.context_gram, f32[256,256]{1,0:T(8,128)S(1)} %get-tuple-element.17.raw), custom_call_target="tpu_custom_call" | custom-call | tf_op jit(solution)/shard_map/update_items/pallas_call | solution.py:371
  248.1 0.7 copy.13
  248.8 0.7 copy.14
Async XLA Ops:
  2.4 2.2 copy-start.1
  4.6 0.9 copy-start.3
  5.6 33.0 %copy-start.2 = (f32[1,1,128,512]{3,2,1,0:T(8,128)S(1)}, f32[1,1,128,512]{3,2,1,0:T(8,128)}, u32[]{:S(2)}) copy-start(f32[1,1,128,512]{3,2,1,0:T(8,128)} %param.15) | copy-start | bytes 786436
  5.6 33.0 %copy-start.4 = (s32[1,1,128]{2,1,0:T(1,128)S(1)}, s32[1,1,128]{2,1,0:T(1,128)}, u32[]{:S(2)}) copy-start(s32[1,1,128]{2,1,0:T(1,128)} %param.12) | copy-start | bytes 1540
  5.6 33.0 %copy-start.5 = (s32[1,1,128]{2,1,0:T(1,128)S(1)}, s32[1,1,128]{2,1,0:T(1,128)}, u32[]{:S(2)}) copy-start(s32[1,1,128]{2,1,0:T(1,128)} %param.11) | copy-start | bytes 1540
  5.6 33.0 %copy-start.6 = (s32[1,1,128]{2,1,0:T(1,128)S(1)}, s32[1,1,128]{2,1,0:T(1,128)}, u32[]{:S(2)}) copy-start(s32[1,1,128]{2,1,0:T(1,128)} %param.13) | copy-start | bytes 1540
  37.2 1.3 copy-start

commit v2 on v1

v2 whole, which is shorter than its diff:
```python
import functools
import math

import jax
import jax.numpy as jnp
from jax import lax
from jax.experimental import pallas as pl
from jax.experimental.pallas import tpu as pltpu
from jax.sharding import PartitionSpec as P

TILE = 64
UNROLL = 32
PAIR = 2 * TILE
BLOCK = 64
PIVOTS = 4
HIGHEST = lax.Precision.HIGHEST
MESH = pl.DeviceIdType.MESH
VMEM_SPEC = pl.BlockSpec(memory_space=pltpu.VMEM)
SMEM_SPEC = pl.BlockSpec(memory_space=pltpu.SMEM)


def dot(left, right):
    return jnp.dot(left, right, precision=HIGHEST, preferred_element_type=jnp.float32)


def gram_of(columns):
    return lax.dot_general(
        columns,
        columns,
        (((1,), (1,)), ((), ())),
        precision=HIGHEST,
        preferred_element_type=jnp.float32,
    )


def mttkrp_kernel(
    target_at,
    count,
    target_ids,
    source_ids,
    context_ids,
    offsets,
    values,
    source,
    context,
    out,
    totals,
):
    totals[...] = jnp.zeros_like(totals)
    rank, entries = totals.shape[2], offsets.shape[2]

    def one_hot(row, extent):
        positions = lax.broadcasted_iota(jnp.int32, (extent, entries), 0)
        return jnp.where(positions == row, 1.0, 0.0).astype(jnp.bfloat16)

    def lanes_of(pair, row):
        wide = pair.astype(jnp.float32)
        picked = [
            jnp.take_along_axis(
                wide,
                jnp.broadcast_to(row[:, at : at + PAIR], (rank, PAIR)),
                axis=1,
                mode="promise_in_bounds",
            )
            for at in range(0, entries, PAIR)
        ]
        return jnp.concatenate(picked, axis=1)

    def group(step, carry):
        first = pl.multiple_of(step * UNROLL, UNROLL)
        targets = offsets[target_at, pl.ds(first, UNROLL), :]
        sources = offsets[1 - target_at, pl.ds(first, UNROLL), :]
        contexts = offsets[2, pl.ds(first, UNROLL), :]
        weights = values[pl.ds(first, UNROLL), :]
        for at in range(UNROLL):
            row = slice(at, at + 1)
            source_id, context_id = source_ids[first + at], context_ids[first + at]
            source_row = sources[row] + TILE * lax.rem(source_id, 2)
            context_row = contexts[row] + TILE * lax.rem(context_id, 2)
            source_part = jnp.dot(
                source[lax.div(source_id, 2)],
                one_hot(source_row, PAIR),
                preferred_element_type=jnp.float32,
            )
            context_part = lanes_of(context[lax.div(context_id, 2)], context_row)
            weight = jnp.where(first + at < count[0], weights[row], 0.0)
            terms = (weight * source_part * context_part).astype(jnp.bfloat16)
            totals[target_ids[first + at]] += lax.dot_general(
                one_hot(targets[row], TILE),
                terms,
                (((1,), (1,)), ((), ())),
                preferred_element_type=jnp.float32,
            )
        return carry

    lax.fori_loop(0, (count[0] + UNROLL - 1) // UNROLL, group, 0)
    out[...] = totals[...].astype(out.dtype)


def mttkrp(target_at, count, ids, offsets, values, source_pairs, context_pairs, tiles):
    shape = (tiles, TILE, source_pairs.shape[1])
    return pl.pallas_call(
        functools.partial(mttkrp_kernel, target_at),
        out_shape=jax.ShapeDtypeStruct(shape, jnp.bfloat16),
        in_specs=[SMEM_SPEC] * 4 + [VMEM_SPEC] * 4,
        out_specs=VMEM_SPEC,
        scratch_shapes=[pltpu.VMEM(shape, jnp.float32)],
        compiler_params=pltpu.CompilerParams(vmem_limit_bytes=48 * 2**20),
        name="mttkrp",
    )(
        count,
        ids[target_at],
        ids[1 - target_at],
        ids[2],
        offsets,
        values,
        source_pairs,
        context_pairs,
    )


def greet(groups):
    barrier = pltpu.get_barrier_semaphore()
    total = 0
    for axis, size in groups:
        me = lax.axis_index(axis)
        for ahead in range(1, size):
            pl.semaphore_signal(
                barrier, inc=1, device_id={axis: lax.rem(me + ahead, size)}, device_id_type=MESH
            )
        total += size - 1
    pl.semaphore_wait(barrier, total)


def send_all(axis, size, source, target, sems):
    me = lax.axis_index(axis)
    copies = []
    for ahead in range(1, size):
        peer = lax.rem(me + ahead, size)
        copy = pltpu.make_async_remote_copy(
            src_ref=source(peer, ahead),
            dst_ref=target(me, ahead),
            send_sem=sems.at[0, ahead - 1],
            recv_sem=sems.at[1, ahead - 1],
            device_id={axis: peer},
            device_id_type=MESH,
        )
        copy.start()
        copies.append(copy)
    return copies


def copy_to(source, target, sems, user, item):
    copy = pltpu.make_async_remote_copy(
        src_ref=source,
        dst_ref=target,
        send_sem=sems.at[0],
        recv_sem=sems.at[1],
        device_id=(user, item),
        device_id_type=MESH,
    )
    copy.start()
    return copy


def receive(copies):
    for copy in copies:
        copy.wait_recv()


def rows_of(item, rows):
    return pl.ds(pl.multiple_of(item * rows, rows), rows)


def start_gram_sum(gram, scattered, sems, items):
    rows = scattered.shape[1]
    item = lax.axis_index("item")
    scattered[item] = gram[rows_of(item, rows), :]
    return send_all(
        "item",
        items,
        lambda peer, ahead: gram.at[rows_of(peer, rows)],
        lambda me, ahead: scattered.at[me],
        sems,
    )


def pass_gram_sum(first, scattered, summed, sems, users):
    receive(first)
    user = lax.axis_index("user")
    summed[user] = jnp.sum(scattered[...], axis=0)
    return send_all(
        "user", users, lambda peer, ahead: summed.at[user], lambda me, ahead: summed.at[me], sems
    )


def spread_gram(result, own, sems, items):
    rows = own.shape[0]
    span = rows_of(lax.axis_index("item"), rows)
    result[span, :] = own[...]
    return send_all("item", items, lambda peer, ahead: own, lambda me, ahead: result.at[span], sems)


def gram_scratch(axis_sizes, width):
    users, items = axis_sizes
    rows = width // items
    return [
        pltpu.VMEM((width, width), jnp.float32),
        pltpu.VMEM((items, rows, width), jnp.float32),
        pltpu.VMEM((users, rows, width), jnp.float32),
        pltpu.SemaphoreType.DMA((2, items - 1)),
        pltpu.SemaphoreType.DMA((2, users - 1)),
        pltpu.SemaphoreType.DMA((2, items - 1)),
    ]


def small_inverse(matrix):
    size = len(matrix)
    if size == 2:
        (first, off), (_, last) = matrix
        scale = 1.0 / (first * last - off * off)
        cross = -off * scale
        return [[last * scale, cross], [cross, first * scale]]
    half = size // 2

    def product(left, right):
        return [
            [sum(left[i][k] * right[k][j] for k in range(1, half)) + left[i][0] * right[0][j] for j in range(half)]
            for i in range(half)
        ]

    corner = small_inverse([row[:half] for row in matrix[:half]])
    side = [row[half:] for row in matrix[:half]]
    solved = product(corner, side)
    lowered = product([list(column) for column in zip(*side)], solved)
    rest = small_inverse(
        [[matrix[half + i][half + j] - lowered[i][j] for j in range(half)] for i in range(half)]
    )
    spread = product(solved, rest)
    update = product(spread, [list(column) for column in zip(*solved)])
    top = [
        [corner[i][j] + update[i][j] for j in range(half)] + [-spread[i][j] for j in range(half)]
        for i in range(half)
    ]
    bottom = [[-spread[j][i] for j in range(half)] + rest[i] for i in range(half)]
    return top + bottom


def invert(work, first_block, last_block):
    width = work.shape[0]
    down = lax.broadcasted_iota(jnp.int32, (BLOCK, BLOCK), 0)
    across = lax.broadcasted_iota(jnp.int32, (BLOCK, BLOCK), 1)
    lanes = lax.broadcasted_iota(jnp.int32, (BLOCK, width), 1) // BLOCK
    rows = lax.broadcasted_iota(jnp.int32, (width, BLOCK), 0) // BLOCK
    full_lanes = lax.broadcasted_iota(jnp.int32, (width, width), 1) // BLOCK
    steps = range(PIVOTS)
    for block in range(first_block, last_block):
        span = slice(block * BLOCK, (block + 1) * BLOCK)
        pivot = work[span, span]
        for at in range(0, BLOCK, PIVOTS):
            columns = [
                jnp.broadcast_to(pivot[:, at + i : at + i + 1], (BLOCK, BLOCK)) for i in steps
            ]
            inverse = small_inverse(
                [
                    [columns[max(i, j)][at + min(i, j) : at + min(i, j) + 1, :] for j in steps]
                    for i in steps
                ]
            )
            fresh = []
            for i in steps:
                row = inverse[i][0] * pivot[at : at + 1, :]
                for j in steps[1:]:
                    row = row + inverse[i][j] * pivot[at + j : at + j + 1, :]
                for j in steps:
                    row = jnp.where(across[:1] == at + j, inverse[i][j], row)
                fresh.append(row)
            after = jnp.where((across >= at) & (across < at + PIVOTS), 0.0, pivot)
            for i in steps:
                after = after - columns[i] * fresh[i]
            for i in steps:
                after = jnp.where(down == at + i, fresh[i], after)
            pivot = after
        panel = dot(pivot, work[span, :])
        panel = jnp.where(lanes == block, jnp.concatenate([pivot] * (width // BLOCK), axis=1), panel)
        column = jnp.where(rows == block, 0.0, work[:, span])
        kept = jnp.where(full_lanes == block, 0.0, work[...])
        work[...] = kept - dot(column, panel)
        work[span, :] = panel


def gather_kernel(
    axis_sizes, step_rows, item_factor, context_factor, items, context, gram_rows, context_gram,
    loaded, gram, scattered, summed, sum_sems, pass_sems, spread_sems, load_sems, own_sems, sibling_sems
):
    users, items_extent = axis_sizes
    user, item = lax.axis_index("user"), lax.axis_index("item")
    steps = context_factor.shape[0] // step_rows
    pairs = step_rows // PAIR

    def load(step):
        span = pl.ds(pl.multiple_of(step * step_rows, step_rows), step_rows)
        return pltpu.make_async_copy(context_factor.at[span], loaded.at[step], load_sems.at[step])

    def transform(step, carry):
        load(step).wait()
        chunk = loaded[step]
        columns = chunk.T
        for pair in range(pairs):
            context[step * pairs + pair] = columns[:, pair * PAIR : (pair + 1) * PAIR].astype(
                jnp.bfloat16
            )
        context_gram[...] += gram_of(columns)
        return carry

    for step in range(steps):
        load(step).start()
    context_gram[...] = jnp.zeros_like(context_gram)
    columns = item_factor[...].T
    for pair in range(items.shape[1]):
        items[user, pair] = columns[:, pair * PAIR : (pair + 1) * PAIR].astype(jnp.bfloat16)
    gram[...] = gram_of(columns)
    greet((("user", users), ("item", items_extent)))
    core = lax.rem(user, 2)
    sibling = user + 1 - 2 * core
    first = start_gram_sum(gram, scattered, sum_sems, items_extent)
    own = []
    for at, ahead in enumerate(range(2, users, 2)):
        peer = lax.rem(user + ahead, users)
        own.append(copy_to(items.at[user], items.at[user], own_sems.at[at], peer, item))
    forwarded = [copy_to(items.at[user], items.at[user], sibling_sems.at[0], sibling, item)]
    lax.fori_loop(0, steps // 2, transform, 0)
    for at, ahead in enumerate(range(2, users, 2)):
        own[at].wait_recv()
        block = items.at[lax.rem(user + users - ahead, users)]
        forwarded.append(copy_to(block, block, sibling_sems.at[1 + at], sibling, item))
    second = pass_gram_sum(first, scattered, summed, pass_sems, users)
    lax.fori_loop(steps // 2, steps, transform, 0)
    receive(second)
    gram_rows[...] = jnp.sum(summed[...], axis=0)
    receive(forwarded)
    for copy in first + own + forwarded + second:
        copy.wait_send()


def gather_items(item_factor, context_factor, axis_sizes):
    users, items = axis_sizes
    rows, width = item_factor.shape
    contexts = context_factor.shape[0]
    step_rows = 512
    gram, scattered, summed, sum_sems, pass_sems, spread_sems = gram_scratch(axis_sizes, width)
    return pl.pallas_call(
        functools.partial(gather_kernel, axis_sizes, step_rows),
        out_shape=(
            jax.ShapeDtypeStruct((users, rows // PAIR, width, PAIR), jnp.bfloat16),
            jax.ShapeDtypeStruct((contexts // PAIR, width, PAIR), jnp.bfloat16),
            jax.ShapeDtypeStruct((width // items, width), jnp.float32),
            jax.ShapeDtypeStruct((width, width), jnp.float32),
        ),
        in_specs=[VMEM_SPEC, pl.BlockSpec(memory_space=pl.ANY)],
        out_specs=(VMEM_SPEC,) * 4,
        scratch_shapes=[
            pltpu.VMEM((contexts // step_rows, step_rows, width), jnp.float32),
            gram, scattered, summed, sum_sems, pass_sems, spread_sems,
            pltpu.SemaphoreType.DMA((contexts // step_rows,)),
            pltpu.SemaphoreType.DMA((users // 2 - 1, 2)),
            pltpu.SemaphoreType.DMA((users // 2, 2)),
        ],
        compiler_params=pltpu.CompilerParams(
            collective_id=0, has_side_effects=True, vmem_limit_bytes=32 * 2**20
        ),
        name="gather_items",
    )(item_factor, context_factor)


def user_kernel(
    axis_sizes, side, partial, gram_rows, context_gram, raw, gathered, raw_gram, arrived, mixed, settled,
    work, gram, scattered, summed, sum_sems, pass_sems, spread_sems, far_sems, near_sems, out_sems, on_sems,
    system_sems, gram_block,
):
    users, items = axis_sizes
    user, item = lax.axis_index("user"), lax.axis_index("item")
    slow, fast = item // side, lax.rem(item, side)
    half = partial.shape[2] // 2
    hops = (2, 1, 3)
    blocks = work.shape[0] // BLOCK
    greet((("user", users), ("item", items)))
    system = spread_gram(work, gram_rows, system_sems, items)

    def at_slow(ahead):
        return lax.rem(slow + ahead, side) * side + fast

    def at_fast(ahead):
        return slow * side + lax.rem(fast + ahead, side)

    far = []
    for ahead in hops:
        far.append(
            copy_to(
                partial.at[lax.rem(slow + ahead, side), :, pl.ds(0, half)],
                arrived.at[0, ahead - 1],
                far_sems.at[0, ahead - 1],
                user,
                at_slow(ahead),
            )
        )
        far.append(
            copy_to(
                partial.at[:, lax.rem(fast + ahead, side), pl.ds(half, half)],
                arrived.at[1, ahead - 1],
                far_sems.at[1, ahead - 1],
                user,
                at_fast(ahead),
            )
        )
    receive(system)
    work[...] = work[...] * context_gram[...]
    invert(work, 0, blocks // 2)

    def combine(part, where):
        own = partial[slow, where, :half] if part == 0 else partial[where, fast, half:]
        total = own.astype(jnp.float32)
        for ahead in range(side - 1):
            total = total + arrived[part, ahead, where].astype(jnp.float32)
        return total

    near = []
    kept = []
    for part in range(2):
        receive(far[part::2])
        here = fast if part == 0 else slow
        for ahead in hops:
            where = lax.rem(here + ahead, side)
            mixed[part, ahead - 1] = combine(part, where)
            near.append(
                copy_to(
                    mixed.at[part, ahead - 1],
                    settled.at[part, ahead - 1],
                    near_sems.at[part, ahead - 1],
                    user,
                    at_fast(ahead) if part == 0 else at_slow(ahead),
                )
            )
        kept.append(combine(part, here))
    invert(work, blocks // 2, blocks)
    receive(near)
    total = jnp.concatenate(
        [kept[part] + jnp.sum(settled[part], axis=0) for part in range(2)], axis=0
    )
    raw[...] = dot(total, work[...])
    columns = raw[...].T
    for part in range(2):
        gathered[item, part] = columns[:, part * PAIR : (part + 1) * PAIR].astype(jnp.bfloat16)

    onward = []

    def pass_on(block, part, stage):
        for ahead in hops:
            onward.append(
                copy_to(
                    gathered.at[block, part],
                    gathered.at[block, part],
                    on_sems.at[part, stage, ahead - 1],
                    user,
                    at_fast(ahead) if part == 0 else at_slow(ahead),
                )
            )

    outward = []
    for ahead in hops:
        for part in range(2):
            outward.append(
                copy_to(
                    gathered.at[item, part],
                    gathered.at[item, part],
                    out_sems.at[part, ahead - 1],
                    user,
                    at_slow(ahead) if part == 0 else at_fast(ahead),
                )
            )
    gram[...] = gram_of(columns)
    first = start_gram_sum(gram, scattered, sum_sems, items)
    for part in range(2):
        pass_on(item, part, 0)
    for at, ahead in ((1, 1), (2, 3), (0, 2)):
        for part in range(2):
            outward[2 * at + part].wait_recv()
            back = side - ahead
            pass_on(at_slow(back) if part == 0 else at_fast(back), part, ahead)
    second = pass_gram_sum(first, scattered, summed, pass_sems, users)
    receive(second)
    gram_block[...] = jnp.sum(summed[...], axis=0)
    third = spread_gram(raw_gram, gram_block, spread_sems, items)
    receive(onward)
    receive(third)
    for copy in system + far + near + outward + onward + first + second + third:
        copy.wait_send()


def update_users(partial, gram_rows, context_gram, axis_sizes):
    users, items = axis_sizes
    side, _, rows, width = partial.shape
    half = rows // 2
    square = jax.ShapeDtypeStruct((width, width), jnp.float32)
    return pl.pallas_call(
        functools.partial(user_kernel, axis_sizes, side),
        out_shape=(
            jax.ShapeDtypeStruct((rows, width), jnp.float32),
            jax.ShapeDtypeStruct((items, rows // PAIR, width, PAIR), jnp.bfloat16),
            square,
        ),
        in_specs=[VMEM_SPEC] * 3,
        out_specs=(VMEM_SPEC,) * 3,
        scratch_shapes=[
            pltpu.VMEM((2, side - 1, side, half, width), jnp.bfloat16),
            pltpu.VMEM((2, side - 1, half, width), jnp.float32),
            pltpu.VMEM((2, side - 1, half, width), jnp.float32),
            pltpu.VMEM((width, width), jnp.float32),
        ]
        + gram_scratch(axis_sizes, width)
        + [
            pltpu.SemaphoreType.DMA((2, side - 1, 2)),
            pltpu.SemaphoreType.DMA((2, side - 1, 2)),
            pltpu.SemaphoreType.DMA((2, side - 1, 2)),
            pltpu.SemaphoreType.DMA((2, side, side - 1, 2)),
            pltpu.SemaphoreType.DMA((2, items - 1)),
            pltpu.VMEM((width // items, width), jnp.float32),
        ],
        compiler_params=pltpu.CompilerParams(
            collective_id=1, has_side_effects=True, vmem_limit_bytes=40 * 2**20
        ),
        name="update_users",
    )(partial, gram_rows, context_gram)


def item_kernel(
    axis_sizes, partial, raw_gram, context_gram, raw, new_items, user_factor, arrived, work,
    user_sums, item_sums, user_sems, item_sems, sems
):
    users, items = axis_sizes
    user, item = lax.axis_index("user"), lax.axis_index("item")
    greet((("user", users), ("item", items)))
    copies = send_all(
        "user",
        users,
        lambda peer, ahead: partial.at[peer],
        lambda me, ahead: arrived.at[ahead - 1],
        sems,
    )
    width = work.shape[0]
    rows_total = jnp.float32(user_factor.shape[0] * users * items)
    down = lax.broadcasted_iota(jnp.int32, (width, width), 0)
    across = lax.broadcasted_iota(jnp.int32, (width, width), 1)
    diagonal = jnp.where(down == across, raw_gram[...], 0.0)
    scale_row = jnp.sqrt(rows_total / (jnp.sum(diagonal, axis=0, keepdims=True) + 1e-06))
    scale_column = jnp.sqrt(rows_total / (jnp.sum(diagonal, axis=1, keepdims=True) + 1e-06))
    user_factor[...] = raw[...] * scale_row
    work[...] = raw_gram[...] * scale_column * scale_row * context_gram[...]
    invert(work, 0, width // BLOCK)
    total = partial[user].astype(jnp.float32)
    for ahead in range(1, users):
        copies[ahead - 1].wait_recv()
        total = total + arrived[ahead - 1].astype(jnp.float32)
    item_raw = dot(total * scale_row, work[...])
    squares = jnp.sum(item_raw * item_raw, axis=0, keepdims=True)
    user_sums[user] = jnp.broadcast_to(squares, user_sums.shape[1:])
    first = send_all(
        "user", users, lambda peer, ahead: user_sums.at[user], lambda me, ahead: user_sums.at[me], user_sems
    )
    receive(first)
    item_sums[item] = jnp.sum(user_sums[...], axis=0)
    second = send_all(
        "item", items, lambda peer, ahead: item_sums.at[item], lambda me, ahead: item_sums.at[me], item_sems
    )
    receive(second)
    squares = jnp.sum(item_sums[...], axis=0)[:1]
    new_items[...] = item_raw * jnp.sqrt(rows_total / (squares + 1e-06))
    for copy in copies + first + second:
        copy.wait_send()


def update_items(partial, raw_gram, context_gram, raw, axis_sizes):
    users, items = axis_sizes
    _, rows, width = partial.shape
    out = jax.ShapeDtypeStruct((rows, width), jnp.float32)
    return pl.pallas_call(
        functools.partial(item_kernel, axis_sizes),
        out_shape=(out, out),
        in_specs=[VMEM_SPEC] * 4,
        out_specs=(VMEM_SPEC,) * 2,
        scratch_shapes=[
            pltpu.VMEM((users - 1, rows, width), jnp.bfloat16),
            pltpu.VMEM((width, width), jnp.float32),
            pltpu.VMEM((users, 8, width), jnp.float32),
            pltpu.VMEM((items, 8, width), jnp.float32),
            pltpu.SemaphoreType.DMA((2, users - 1)),
            pltpu.SemaphoreType.DMA((2, items - 1)),
            pltpu.SemaphoreType.DMA((2, users - 1)),
        ],
        compiler_params=pltpu.CompilerParams(
            collective_id=2, has_side_effects=True, vmem_limit_bytes=32 * 2**20
        ),
        name="update_items",
    )(partial, raw_gram, context_gram, raw)


def local(
    item_factor, context_factor, tile_count, tile_rows, tile_cols, tile_ctx, nz_offsets, nz_values
):
    axis_sizes = (lax.axis_size("user"), lax.axis_size("item"))
    users, items = axis_sizes
    rows, width = item_factor.shape
    side = math.isqrt(items)
    count = tile_count.reshape(1)
    ids = (tile_rows[0, 0], tile_cols[0, 0], tile_ctx[0, 0])
    offsets = nz_offsets[0, 0]
    values = nz_values[0, 0]
    item_pairs, context_pairs, gram_rows, context_gram = gather_items(
        item_factor, context_factor, axis_sizes
    )
    partial_users = mttkrp(
        0, count, ids, offsets, values, item_pairs.reshape(-1, width, PAIR), context_pairs,
        items * rows // TILE,
    )
    raw, user_pairs, raw_gram = update_users(
        partial_users.reshape(side, side, rows, width), gram_rows, context_gram, axis_sizes
    )
    partial_items = mttkrp(
        1, count, ids, offsets, values, user_pairs.reshape(-1, width, PAIR), context_pairs,
        users * rows // TILE,
    )
    new_items, user_factor = update_items(
        partial_items.reshape(users, rows, width), raw_gram, context_gram, raw, axis_sizes
    )
    return (user_factor, new_items)


def solution(mesh):
    in_specs = (
        P(("item", "user"), None),
        P(),
        P("user", "item"),
        P("user", "item", None),
        P("user", "item", None),
        P("user", "item", None),
        P("user", "item", None, None, None),
        P("user", "item", None, None),
    )
    out_specs = (P(("user", "item"), None), P(("item", "user"), None))
    return jax.shard_map(local, mesh=mesh, in_specs=in_specs, out_specs=out_specs, check_vma=False)
```

time: 250 us -> 152 us (0.61)
  Pallas kernels: 241 us -> 145 us
    pallas_call x4, Pallas kernels: 198 us -> 108 us  [the longest x1 60.8 us: update_users(): pl.pallas_call(functools.partial(user_kernel, axis_sizes, side), out_shap...]
    pallas_call x1, Pallas kernels: 43.3 us -> 37.2 us  [update_items(): pl.pallas_call(functools.partial(item_kernel, axis_sizes), out_shape=(out...]
    unnamed x16 -> x18, local copies, waits for them, and re-layouts: 5.88 us -> 5.88 us
where the time goes in v2:
time: 152 us
  Pallas kernels  145 us (95%)
  local copies, waits for them, and re-layouts  5.88 us (4%)
    pallas_call x1, Pallas kernels, update_users(): pl.pallas_call(functools.partial(user_kernel, axis_sizes, side), out_shap...  60.8 us
    pallas_call x1, Pallas kernels, update_items(): pl.pallas_call(functools.partial(item_kernel, axis_sizes), out_shape=(out...  37.2 us
    pallas_call x2, Pallas kernels, mttkrp(): pl.pallas_call(functools.partial(mttkrp_kernel, target_at), out_shape=jax...  24.2 us
    pallas_call x1, Pallas kernels, gather_items(): pl.pallas_call(functools.partial(gather_kernel, axis_sizes, step_rows), o...  22.5 us
    unnamed x18, local copies, waits for them, and re-layouts  5.88 us

profile of v2, /device:TPU:1, one launch (start us, length us, event | category | flops | bytes accessed | tf_op | source)
XLA Modules:
  0.0 152.0 jit_solution(15291884954701939466)
XLA Ops:
  1.3 0.0 copy-start.1
  1.3 2.2 %copy-done.1 = f32[4096,256]{1,0:T(8,128)S(1)} copy-done((f32[4096,256]{1,0:T(8,128)S(1)}, f32[4096,256]{1,0:T(8,128)}, u32[]{:S(2)}) %copy-start.1) | copy-done | bytes 4194328
  3.5 0.0 copy-start.4
  3.5 0.9 copy-done.4
  4.4 0.0 copy-start.2
  4.4 0.0 copy-start.3
  4.4 0.0 copy-start.5
  4.4 0.0 copy-start.6
  4.4 0.0 copy-start.7
  4.4 22.5 %gather_items.1 = (bf16[8,2,256,128]{3,2,1,0:T(8,128)(2,1)S(1)}, bf16[32,256,128]{2,1,0:T(8,128)(2,1)S(1)}, f32[16,256]{1,0:T(8,128)S(1)}, f32[256,256]{1,0:T(8,128)S(1)}) custom-call(f32[256,256]{1,0:T(8,128)S(1)} %copy-done.4, f32[4096,256]{1,0:T(8,128)S(1)} %copy-done.1), custom_call_target="tpu_custom_call" | custom-call | tf_op jit(solution)/shard_map/gather_items/pallas_call | solution.py:352
  26.9 0.0 copy-start
  27.0 1.3 copy-done
  28.3 0.0 copy-done.2
  28.3 0.0 copy-done.3
  28.3 0.0 copy-done.5
  28.3 0.0 copy-done.6
  28.3 0.0 copy-done.7
  28.3 12.2 %mttkrp.2 = bf16[64,64,256]{2,1,0:T(8,128)(2,1)S(1)} custom-call(s32[1]{0:T(128)} %bitcast.10.count, s32[128]{0:T(128)S(1)} %bitcast.22, s32[128]{0:T(128)S(1)} %bitcast.20, s32[128]{0:T(128)S(1)} %bitcast.24, s32[3,128,512]{2,1,0:T(8,128)S(1)} %bitcast.14, f32[128,512]{1,0:T(8,128)S(1)} %bitcast.17, bf16[16,256,128]{2,1,0:T(8,128)(2,1)S(1)} %bitcast.19, ...), custom_call_target="tpu_custom_call" | custom-call | tf_op jit(solution)/shard_map/mttkrp/pallas_call | solution.py:102
  40.5 60.8 %update_users.1 = (f32[256,256]{1,0:T(8,128)S(1)}, bf16[16,2,256,128]{3,2,1,0:T(8,128)(2,1)S(1)}, f32[256,256]{1,0:T(8,128)S(1)}) custom-call(bf16[4,4,256,256]{3,2,1,0:T(8,128)(2,1)S(1)} %bitcast.12, f32[16,256]{1,0:T(8,128)S(1)} %get-tuple-element.13.gram_rows, f32[256,256]{1,0:T(8,128)S(1)} %get-tuple-element.14.context_gram), custom_call_target="tpu_custom_call" | custom-call | tf_op jit(solution)/shard_map/update_users/pallas_call | solution.py:505
  101.3 12.1 %mttkrp.3 = bf16[32,64,256]{2,1,0:T(8,128)(2,1)S(1)} custom-call(s32[1]{0:T(128)} %bitcast.11.count, s32[128]{0:T(128)S(1)} %bitcast.21, s32[128]{0:T(128)S(1)} %bitcast.23, s32[128]{0:T(128)S(1)} %bitcast.25, s32[3,128,512]{2,1,0:T(8,128)S(1)} %bitcast.15, f32[128,512]{1,0:T(8,128)S(1)} %bitcast.18, bf16[32,256,128]{2,1,0:T(8,128)(2,1)S(1)} %bitcast.16, ...), custom_call_target="tpu_custom_call" | custom-call | tf_op jit(solution)/shard_map/mttkrp/pallas_call | solution.py:102
  113.3 37.2 %update_items.1 = (f32[256,256]{1,0:T(8,128)S(1)}, f32[256,256]{1,0:T(8,128)S(1)}) custom-call(bf16[8,256,256]{2,1,0:T(8,128)(2,1)S(1)} %bitcast.13, f32[256,256]{1,0:T(8,128)S(1)} %get-tuple-element.16.raw_gram, f32[256,256]{1,0:T(8,128)S(1)} %get-tuple-element.14.context_gram, f32[256,256]{1,0:T(8,128)S(1)} %get-tuple-element.17.raw), custom_call_target="tpu_custom_call" | custom-call | tf_op jit(solution)/shard_map/update_items/pallas_call | solution.py:586
  150.6 0.7 copy.13
  151.3 0.7 copy.14
Async XLA Ops:
  1.3 2.2 %copy-start.1 = (f32[4096,256]{1,0:T(8,128)S(1)}, f32[4096,256]{1,0:T(8,128)}, u32[]{:S(2)}) copy-start(f32[4096,256]{1,0:T(8,128)} %context_factor.1) | copy-start | bytes 12582916
  3.5 0.9 copy-start.4
  4.4 23.9 %copy-start.2 = (s32[1,1,3,128,512]{4,3,2,1,0:T(8,128)S(1)}, s32[1,1,3,128,512]{4,3,2,1,0:T(8,128)}, u32[]{:S(2)}) copy-start(s32[1,1,3,128,512]{4,3,2,1,0:T(8,128)} %param.14) | copy-start | bytes 2359300
  4.4 23.9 %copy-start.3 = (f32[1,1,128,512]{3,2,1,0:T(8,128)S(1)}, f32[1,1,128,512]{3,2,1,0:T(8,128)}, u32[]{:S(2)}) copy-start(f32[1,1,128,512]{3,2,1,0:T(8,128)} %param.15) | copy-start | bytes 786436
  4.4 23.9 %copy-start.5 = (s32[1,1,128]{2,1,0:T(1,128)S(1)}, s32[1,1,128]{2,1,0:T(1,128)}, u32[]{:S(2)}) copy-start(s32[1,1,128]{2,1,0:T(1,128)} %param.12) | copy-start | bytes 1540
  4.4 23.9 %copy-start.6 = (s32[1,1,128]{2,1,0:T(1,128)S(1)}, s32[1,1,128]{2,1,0:T(1,128)}, u32[]{:S(2)}) copy-start(s32[1,1,128]{2,1,0:T(1,128)} %param.11) | copy-start | bytes 1540
  4.4 23.9 %copy-start.7 = (s32[1,1,128]{2,1,0:T(1,128)S(1)}, s32[1,1,128]{2,1,0:T(1,128)}, u32[]{:S(2)}) copy-start(s32[1,1,128]{2,1,0:T(1,128)} %param.13) | copy-start | bytes 1540
  26.9 1.3 copy-start

commit v3 on v2

--- a/solution.py
+++ b/solution.py
@@ -105,7 +105,7 @@
         in_specs=[SMEM_SPEC] * 4 + [VMEM_SPEC] * 4,
         out_specs=VMEM_SPEC,
         scratch_shapes=[pltpu.VMEM(shape, jnp.float32)],
-        compiler_params=pltpu.CompilerParams(vmem_limit_bytes=48 * 2**20),
+        compiler_params=pltpu.CompilerParams(vmem_limit_bytes=24 * 2**20),
         name="mttkrp",
     )(
         count,
@@ -121,15 +121,16 @@
 
 def greet(groups):
     barrier = pltpu.get_barrier_semaphore()
-    total = 0
     for axis, size in groups:
         me = lax.axis_index(axis)
         for ahead in range(1, size):
             pl.semaphore_signal(
                 barrier, inc=1, device_id={axis: lax.rem(me + ahead, size)}, device_id_type=MESH
             )
-        total += size - 1
-    pl.semaphore_wait(barrier, total)
+
+
+def await_greetings(groups):
+    pl.semaphore_wait(pltpu.get_barrier_semaphore(), sum(size - 1 for _, size in groups))
 
 
 def send_all(axis, size, source, target, sems):
@@ -172,45 +173,91 @@
     return pl.ds(pl.multiple_of(item * rows, rows), rows)
 
 
-def start_gram_sum(gram, scattered, sems, items):
-    rows = scattered.shape[1]
+def gram_to_users(gram, by_user, sems, users):
+    rows = by_user.shape[1]
+    user = lax.axis_index("user")
+    by_user[user] = gram[rows_of(user, rows), :]
+    return send_all(
+        "user",
+        users,
+        lambda peer, ahead: gram.at[rows_of(peer, rows)],
+        lambda me, ahead: by_user.at[me],
+        sems,
+    )
+
+
+def gram_to_items(first, by_user, pieces, by_item, sems, items):
+    receive(first)
+    block = jnp.sum(by_user[...], axis=0)
+    count = pieces.shape[0]
+    for piece in range(count):
+        pieces[piece] = piece_of(block, piece)
     item = lax.axis_index("item")
-    scattered[item] = gram[rows_of(item, rows), :]
+    by_item[item] = pieces[lax.rem(item, count)]
     return send_all(
         "item",
         items,
-        lambda peer, ahead: gram.at[rows_of(peer, rows)],
-        lambda me, ahead: scattered.at[me],
+        lambda peer, ahead: pieces.at[lax.rem(peer, count)],
+        lambda me, ahead: by_item.at[me],
         sems,
     )
 
 
-def pass_gram_sum(first, scattered, summed, sems, users):
-    receive(first)
-    user = lax.axis_index("user")
-    summed[user] = jnp.sum(scattered[...], axis=0)
-    return send_all(
-        "user", users, lambda peer, ahead: summed.at[user], lambda me, ahead: summed.at[me], sems
-    )
-
-
-def spread_gram(result, own, sems, items):
-    rows = own.shape[0]
-    span = rows_of(lax.axis_index("item"), rows)
-    result[span, :] = own[...]
-    return send_all("item", items, lambda peer, ahead: own, lambda me, ahead: result.at[span], sems)
-
-
-def gram_scratch(axis_sizes, width):
+def piece_of(block, piece):
+    down, across = 8 * (piece // 2), 128 * (piece % 2)
+    return block[down : down + 8, across : across + 128]
+
+
+def pieces_back(own, finished, sems):
+    count = finished.shape[0]
+    user, item = lax.axis_index("user"), lax.axis_index("item")
+    at = lax.rem(item, count)
+    finished[at] = own[...]
+    return [
+        copy_to(
+            own,
+            finished.at[at],
+            sems.at[ahead - 1],
+            user,
+            item - at + lax.rem(at + ahead, count),
+        )
+        for ahead in range(1, count)
+    ]
+
+
+def blocks_back(third, finished, block, result, sems, users):
+    receive(third)
+    for piece in range(finished.shape[0]):
+        down, across = 8 * (piece // 2), 128 * (piece % 2)
+        block[down : down + 8, across : across + 128] = finished[piece]
+    rows = block.shape[0]
+    span = rows_of(lax.axis_index("user"), rows)
+    result[span, :] = block[...]
+    return send_all("user", users, lambda peer, ahead: block, lambda me, ahead: result.at[span], sems)
+
+
+def gram_sum_scratch(axis_sizes, width):
     users, items = axis_sizes
-    rows = width // items
+    rows = width // users
     return [
         pltpu.VMEM((width, width), jnp.float32),
-        pltpu.VMEM((items, rows, width), jnp.float32),
         pltpu.VMEM((users, rows, width), jnp.float32),
-        pltpu.SemaphoreType.DMA((2, items - 1)),
+        pltpu.VMEM((rows * width // 1024, 8, 128), jnp.float32),
+        pltpu.VMEM((items, 8, 128), jnp.float32),
         pltpu.SemaphoreType.DMA((2, users - 1)),
         pltpu.SemaphoreType.DMA((2, items - 1)),
+    ]
+
+
+def gram_spread_scratch(axis_sizes, width):
+    users, items = axis_sizes
+    rows = width // users
+    count = rows * width // 1024
+    return [
+        pltpu.VMEM((count, 8, 128), jnp.float32),
+        pltpu.VMEM((rows, width), jnp.float32),
+        pltpu.SemaphoreType.DMA((count - 1, 2)),
+        pltpu.SemaphoreType.DMA((2, users - 1)),
     ]
 
 
@@ -290,13 +337,15 @@
 
 
 def gather_kernel(
-    axis_sizes, step_rows, item_factor, context_factor, items, context, gram_rows, context_gram,
-    loaded, gram, scattered, summed, sum_sems, pass_sems, spread_sems, load_sems, own_sems, sibling_sems
+    axis_sizes, step_rows, item_factor, context_factor, items, context, gram_piece, context_gram,
+    loaded, load_sems, own_sems, sibling_sems, gram, by_user, pieces, by_item, user_sems, item_sems,
 ):
     users, items_extent = axis_sizes
+    everyone = (("user", users), ("item", items_extent))
     user, item = lax.axis_index("user"), lax.axis_index("item")
     steps = context_factor.shape[0] // step_rows
     pairs = step_rows // PAIR
+    greet(everyone)
 
     def load(step):
         span = pl.ds(pl.multiple_of(step * step_rows, step_rows), step_rows)
@@ -320,24 +369,24 @@
     for pair in range(items.shape[1]):
         items[user, pair] = columns[:, pair * PAIR : (pair + 1) * PAIR].astype(jnp.bfloat16)
     gram[...] = gram_of(columns)
-    greet((("user", users), ("item", items_extent)))
+    await_greetings(everyone)
     core = lax.rem(user, 2)
     sibling = user + 1 - 2 * core
-    first = start_gram_sum(gram, scattered, sum_sems, items_extent)
     own = []
     for at, ahead in enumerate(range(2, users, 2)):
         peer = lax.rem(user + ahead, users)
         own.append(copy_to(items.at[user], items.at[user], own_sems.at[at], peer, item))
     forwarded = [copy_to(items.at[user], items.at[user], sibling_sems.at[0], sibling, item)]
-    lax.fori_loop(0, steps // 2, transform, 0)
+    first = gram_to_users(gram, by_user, user_sems, users)
+    lax.fori_loop(0, steps // 4, transform, 0)
     for at, ahead in enumerate(range(2, users, 2)):
         own[at].wait_recv()
         block = items.at[lax.rem(user + users - ahead, users)]
         forwarded.append(copy_to(block, block, sibling_sems.at[1 + at], sibling, item))
-    second = pass_gram_sum(first, scattered, summed, pass_sems, users)
-    lax.fori_loop(steps // 2, steps, transform, 0)
+    second = gram_to_items(first, by_user, pieces, by_item, item_sems, items_extent)
+    lax.fori_loop(steps // 4, steps, transform, 0)
     receive(second)
-    gram_rows[...] = jnp.sum(summed[...], axis=0)
+    gram_piece[...] = jnp.sum(by_item[...], axis=0)
     receive(forwarded)
     for copy in first + own + forwarded + second:
         copy.wait_send()
@@ -348,35 +397,35 @@
     rows, width = item_factor.shape
     contexts = context_factor.shape[0]
     step_rows = 512
-    gram, scattered, summed, sum_sems, pass_sems, spread_sems = gram_scratch(axis_sizes, width)
     return pl.pallas_call(
         functools.partial(gather_kernel, axis_sizes, step_rows),
         out_shape=(
             jax.ShapeDtypeStruct((users, rows // PAIR, width, PAIR), jnp.bfloat16),
             jax.ShapeDtypeStruct((contexts // PAIR, width, PAIR), jnp.bfloat16),
-            jax.ShapeDtypeStruct((width // items, width), jnp.float32),
+            jax.ShapeDtypeStruct((8, 128), jnp.float32),
             jax.ShapeDtypeStruct((width, width), jnp.float32),
         ),
-        in_specs=[VMEM_SPEC, pl.BlockSpec(memory_space=pl.ANY)],
+        in_specs=[VMEM_SPEC, pl.BlockSpec(memory_space=pltpu.HBM)],
         out_specs=(VMEM_SPEC,) * 4,
         scratch_shapes=[
             pltpu.VMEM((contexts // step_rows, step_rows, width), jnp.float32),
-            gram, scattered, summed, sum_sems, pass_sems, spread_sems,
             pltpu.SemaphoreType.DMA((contexts // step_rows,)),
             pltpu.SemaphoreType.DMA((users // 2 - 1, 2)),
             pltpu.SemaphoreType.DMA((users // 2, 2)),
-        ],
+        ]
+        + gram_sum_scratch(axis_sizes, width),
         compiler_params=pltpu.CompilerParams(
-            collective_id=0, has_side_effects=True, vmem_limit_bytes=32 * 2**20
+            collective_id=0, has_side_effects=True, vmem_limit_bytes=16 * 2**20
         ),
         name="gather_items",
     )(item_factor, context_factor)
 
 
 def user_kernel(
-    axis_sizes, side, partial, gram_rows, context_gram, raw, gathered, raw_gram, arrived, mixed, settled,
-    work, gram, scattered, summed, sum_sems, pass_sems, spread_sems, far_sems, near_sems, out_sems, on_sems,
-    system_sems, gram_block,
+    axis_sizes, side, partial, gram_piece, context_gram, raw, gathered, raw_gram, arrived, mixed, settled,
+    work, raw_piece, far_sems, near_sems, out_sems, on_sems,
+    gram, by_user, pieces, by_item, user_sems, item_sems,
+    finished, gram_block, piece_sems, block_sems, raw_finished, raw_block, raw_piece_sems, raw_block_sems,
 ):
     users, items = axis_sizes
     user, item = lax.axis_index("user"), lax.axis_index("item")
@@ -384,8 +433,10 @@
     half = partial.shape[2] // 2
     hops = (2, 1, 3)
     blocks = work.shape[0] // BLOCK
-    greet((("user", users), ("item", items)))
-    system = spread_gram(work, gram_rows, system_sems, items)
+    everyone = (("user", users), ("item", items))
+    greet(everyone)
+    await_greetings(everyone)
+    third = pieces_back(gram_piece, finished, piece_sems)
 
     def at_slow(ahead):
         return lax.rem(slow + ahead, side) * side + fast
@@ -413,7 +464,8 @@
                 at_fast(ahead),
             )
         )
-    receive(system)
+    fourth = blocks_back(third, finished, gram_block, work, block_sems, users)
+    receive(fourth)
     work[...] = work[...] * context_gram[...]
     invert(work, 0, blocks // 2)
 
@@ -431,7 +483,7 @@
         here = fast if part == 0 else slow
         for ahead in hops:
             where = lax.rem(here + ahead, side)
-            mixed[part, ahead - 1] = combine(part, where)
+            mixed[part, ahead - 1] = combine(part, where).astype(mixed.dtype)
             near.append(
                 copy_to(
                     mixed.at[part, ahead - 1],
@@ -445,7 +497,11 @@
     invert(work, blocks // 2, blocks)
     receive(near)
     total = jnp.concatenate(
-        [kept[part] + jnp.sum(settled[part], axis=0) for part in range(2)], axis=0
+        [
+            kept[part] + sum(settled[part, at].astype(jnp.float32) for at in range(side - 1))
+            for part in range(2)
+        ],
+        axis=0,
     )
     raw[...] = dot(total, work[...])
     columns = raw[...].T
@@ -479,7 +535,7 @@
                 )
             )
     gram[...] = gram_of(columns)
-    first = start_gram_sum(gram, scattered, sum_sems, items)
+    first = gram_to_users(gram, by_user, user_sems, users)
     for part in range(2):
         pass_on(item, part, 0)
     for at, ahead in ((1, 1), (2, 3), (0, 2)):
@@ -487,17 +543,18 @@
             outward[2 * at + part].wait_recv()
             back = side - ahead
             pass_on(at_slow(back) if part == 0 else at_fast(back), part, ahead)
-    second = pass_gram_sum(first, scattered, summed, pass_sems, users)
+    second = gram_to_items(first, by_user, pieces, by_item, item_sems, items)
     receive(second)
-    gram_block[...] = jnp.sum(summed[...], axis=0)
-    third = spread_gram(raw_gram, gram_block, spread_sems, items)
+    raw_piece[...] = jnp.sum(by_item[...], axis=0)
+    fifth = pieces_back(raw_piece, raw_finished, raw_piece_sems)
+    sixth = blocks_back(fifth, raw_finished, raw_block, raw_gram, raw_block_sems, users)
     receive(onward)
-    receive(third)
-    for copy in system + far + near + outward + onward + first + second + third:
+    receive(sixth)
+    for copy in third + fourth + far + near + outward + onward + first + second + fifth + sixth:
         copy.wait_send()
 
 
-def update_users(partial, gram_rows, context_gram, axis_sizes):
+def update_users(partial, gram_piece, context_gram, axis_sizes):
     users, items = axis_sizes
     side, _, rows, width = partial.shape
     half = rows // 2
@@ -513,24 +570,23 @@
         out_specs=(VMEM_SPEC,) * 3,
         scratch_shapes=[
             pltpu.VMEM((2, side - 1, side, half, width), jnp.bfloat16),
-            pltpu.VMEM((2, side - 1, half, width), jnp.float32),
-            pltpu.VMEM((2, side - 1, half, width), jnp.float32),
+            pltpu.VMEM((2, side - 1, half, width), jnp.bfloat16),
+            pltpu.VMEM((2, side - 1, half, width), jnp.bfloat16),
             pltpu.VMEM((width, width), jnp.float32),
-        ]
-        + gram_scratch(axis_sizes, width)
-        + [
+            pltpu.VMEM((8, 128), jnp.float32),
             pltpu.SemaphoreType.DMA((2, side - 1, 2)),
             pltpu.SemaphoreType.DMA((2, side - 1, 2)),
             pltpu.SemaphoreType.DMA((2, side - 1, 2)),
             pltpu.SemaphoreType.DMA((2, side, side - 1, 2)),
-            pltpu.SemaphoreType.DMA((2, items - 1)),
-            pltpu.VMEM((width // items, width), jnp.float32),
-        ],
+        ]
+        + gram_sum_scratch(axis_sizes, width)
+        + gram_spread_scratch(axis_sizes, width)
+        + gram_spread_scratch(axis_sizes, width),
         compiler_params=pltpu.CompilerParams(
-            collective_id=1, has_side_effects=True, vmem_limit_bytes=40 * 2**20
+            collective_id=1, has_side_effects=True, vmem_limit_bytes=24 * 2**20
         ),
         name="update_users",
-    )(partial, gram_rows, context_gram)
+    )(partial, gram_piece, context_gram)
 
 
 def item_kernel(
@@ -539,7 +595,9 @@
 ):
     users, items = axis_sizes
     user, item = lax.axis_index("user"), lax.axis_index("item")
-    greet((("user", users), ("item", items)))
+    everyone = (("user", users), ("item", items))
+    greet(everyone)
+    await_greetings(everyone)
     copies = send_all(
         "user",
         users,
@@ -598,7 +656,7 @@
             pltpu.SemaphoreType.DMA((2, users - 1)),
         ],
         compiler_params=pltpu.CompilerParams(
-            collective_id=2, has_side_effects=True, vmem_limit_bytes=32 * 2**20
+            collective_id=2, has_side_effects=True, vmem_limit_bytes=16 * 2**20
         ),
         name="update_items",
     )(partial, raw_gram, context_gram, raw)
@@ -615,7 +673,7 @@
     ids = (tile_rows[0, 0], tile_cols[0, 0], tile_ctx[0, 0])
     offsets = nz_offsets[0, 0]
     values = nz_values[0, 0]
-    item_pairs, context_pairs, gram_rows, context_gram = gather_items(
+    item_pairs, context_pairs, gram_piece, context_gram = gather_items(
         item_factor, context_factor, axis_sizes
     )
     partial_users = mttkrp(
@@ -623,7 +681,7 @@
         items * rows // TILE,
     )
     raw, user_pairs, raw_gram = update_users(
-        partial_users.reshape(side, side, rows, width), gram_rows, context_gram, axis_sizes
+        partial_users.reshape(side, side, rows, width), gram_piece, context_gram, axis_sizes
     )
     partial_items = mttkrp(
         1, count, ids, offsets, values, user_pairs.reshape(-1, width, PAIR), context_pairs,

time: 152 us -> 157 us (1.033)
  Pallas kernels: 145 us -> 150 us
    pallas_call x1, Pallas kernels: 60.8 us -> 73 us  [update_users(): pl.pallas_call(functools.partial(user_kernel, axis_sizes, side), out_shap...]
    pallas_call x2, Pallas kernels: 24.2 us -> 12.1 us  [mttkrp(): pl.pallas_call(functools.partial(mttkrp_kernel, target_at), out_shape=jax...]
    pallas_call x1, Pallas kernels: 37.2 us -> 40.4 us  [update_items(): pl.pallas_call(functools.partial(item_kernel, axis_sizes), out_shape=(out...]
    pallas_call x1, Pallas kernels: 22.5 us -> 24.9 us  [gather_items(): pl.pallas_call(functools.partial(gather_kernel, axis_sizes, step_rows), o...]
    unnamed x18 -> x16, local copies, waits for them, and re-layouts: 5.88 us -> 4.56 us
where the time goes in v3:
time: 157 us; the launch traced here: 156 us
  Pallas kernels  150 us (96%)
  local copies, waits for them, and re-layouts  4.56 us (3%)
    pallas_call x1, Pallas kernels, update_users(): pl.pallas_call(functools.partial(user_kernel, axis_sizes, side), out_shap...  73 us
    pallas_call x1, Pallas kernels, update_items(): pl.pallas_call(functools.partial(item_kernel, axis_sizes), out_shape=(out...  40.4 us
    pallas_call x1, Pallas kernels, gather_items(): pl.pallas_call(functools.partial(gather_kernel, axis_sizes, step_rows), o...  24.9 us
    pallas_call x2, Pallas kernels, mttkrp(): pl.pallas_call(functools.partial(mttkrp_kernel, target_at), out_shape=jax...  12.1 us
    unnamed x16, local copies, waits for them, and re-layouts  4.56 us

profile of v3, /device:TPU:1, one launch (start us, length us, event | category | flops | bytes accessed | tf_op | source)
XLA Modules:
  0.0 156.4 jit_solution(14714798474602479731)
XLA Ops:
  1.3 0.0 copy-start
  1.3 2.2 %copy-done = f32[4096,256]{1,0:T(8,128)S(1)} copy-done((f32[4096,256]{1,0:T(8,128)S(1)}, f32[4096,256]{1,0:T(8,128)}, u32[]{:S(2)}) %copy-start) | copy-done | bytes 4194328
  3.5 0.0 copy-start.3
  3.5 0.9 copy-done.3
  4.4 0.0 copy-start.1
  4.4 0.0 copy-start.2
  4.4 0.0 copy-start.4
  4.4 0.0 copy-start.5
  4.4 0.0 copy-start.6
  4.4 24.9 %gather_items.1 = (bf16[8,2,256,128]{3,2,1,0:T(8,128)(2,1)S(1)}, bf16[32,256,128]{2,1,0:T(8,128)(2,1)S(1)}, f32[8,128]{1,0:T(8,128)S(1)}, f32[256,256]{1,0:T(8,128)S(1)}) custom-call(f32[256,256]{1,0:T(8,128)S(1)} %copy-done.3, f32[4096,256]{1,0:T(8,128)S(1)} %copy-done), custom_call_target="tpu_custom_call" | custom-call | tf_op jit(solution)/shard_map/gather_items/pallas_call | solution.py:400
  29.4 0.0 copy-done.1
  29.4 0.0 copy-done.2
  29.4 0.0 copy-done.4
  29.4 0.0 copy-done.5
  29.4 0.0 copy-done.6
  29.4 6.1 %mttkrp.2 = bf16[64,64,256]{2,1,0:T(8,128)(2,1)S(1)} custom-call(s32[1]{0:T(128)} %bitcast.10.count, s32[128]{0:T(128)S(1)} %bitcast.22, s32[128]{0:T(128)S(1)} %bitcast.20, s32[128]{0:T(128)S(1)} %bitcast.24, s32[3,128,512]{2,1,0:T(8,128)S(1)} %bitcast.14, f32[128,512]{1,0:T(8,128)S(1)} %bitcast.17, bf16[16,256,128]{2,1,0:T(8,128)(2,1)S(1)} %bitcast.19, ...), custom_call_target="tpu_custom_call" | custom-call | tf_op jit(solution)/shard_map/mttkrp/pallas_call | solution.py:102
  35.6 73.0 %update_users.1 = (f32[256,256]{1,0:T(8,128)S(1)}, bf16[16,2,256,128]{3,2,1,0:T(8,128)(2,1)S(1)}, f32[256,256]{1,0:T(8,128)S(1)}) custom-call(bf16[4,4,256,256]{3,2,1,0:T(8,128)(2,1)S(1)} %bitcast.12, f32[8,128]{1,0:T(8,128)S(1)} %get-tuple-element.13.gram_piece, f32[256,256]{1,0:T(8,128)S(1)} %get-tuple-element.14.context_gram), custom_call_target="tpu_custom_call" | custom-call | tf_op jit(solution)/shard_map/update_users/pallas_call | solution.py:562
  108.6 6.0 %mttkrp.3 = bf16[32,64,256]{2,1,0:T(8,128)(2,1)S(1)} custom-call(s32[1]{0:T(128)} %bitcast.11.count, s32[128]{0:T(128)S(1)} %bitcast.21, s32[128]{0:T(128)S(1)} %bitcast.23, s32[128]{0:T(128)S(1)} %bitcast.25, s32[3,128,512]{2,1,0:T(8,128)S(1)} %bitcast.15, f32[128,512]{1,0:T(8,128)S(1)} %bitcast.18, bf16[32,256,128]{2,1,0:T(8,128)(2,1)S(1)} %bitcast.16, ...), custom_call_target="tpu_custom_call" | custom-call | tf_op jit(solution)/shard_map/mttkrp/pallas_call | solution.py:102
  114.5 40.4 %update_items.1 = (f32[256,256]{1,0:T(8,128)S(1)}, f32[256,256]{1,0:T(8,128)S(1)}) custom-call(bf16[8,256,256]{2,1,0:T(8,128)(2,1)S(1)} %bitcast.13, f32[256,256]{1,0:T(8,128)S(1)} %get-tuple-element.16.raw_gram, f32[256,256]{1,0:T(8,128)S(1)} %get-tuple-element.14.context_gram, f32[256,256]{1,0:T(8,128)S(1)} %get-tuple-element.17.raw), custom_call_target="tpu_custom_call" | custom-call | tf_op jit(solution)/shard_map/update_items/pallas_call | solution.py:644
  154.9 0.7 copy.13
  155.7 0.7 copy.14
Async XLA Ops:
  1.3 2.2 %copy-start = (f32[4096,256]{1,0:T(8,128)S(1)}, f32[4096,256]{1,0:T(8,128)}, u32[]{:S(2)}) copy-start(f32[4096,256]{1,0:T(8,128)} %context_factor.1) | copy-start | bytes 12582916
  3.5 0.9 copy-start.3
  4.4 25.0 %copy-start.1 = (s32[1,1,3,128,512]{4,3,2,1,0:T(8,128)S(1)}, s32[1,1,3,128,512]{4,3,2,1,0:T(8,128)}, u32[]{:S(2)}) copy-start(s32[1,1,3,128,512]{4,3,2,1,0:T(8,128)} %param.14) | copy-start | bytes 2359300
  4.4 25.0 %copy-start.2 = (f32[1,1,128,512]{3,2,1,0:T(8,128)S(1)}, f32[1,1,128,512]{3,2,1,0:T(8,128)}, u32[]{:S(2)}) copy-start(f32[1,1,128,512]{3,2,1,0:T(8,128)} %param.15) | copy-start | bytes 786436
  4.4 25.0 %copy-start.4 = (s32[1,1,128]{2,1,0:T(1,128)S(1)}, s32[1,1,128]{2,1,0:T(1,128)}, u32[]{:S(2)}) copy-start(s32[1,1,128]{2,1,0:T(1,128)} %param.12) | copy-start | bytes 1540
  4.4 25.0 %copy-start.5 = (s32[1,1,128]{2,1,0:T(1,128)S(1)}, s32[1,1,128]{2,1,0:T(1,128)}, u32[]{:S(2)}) copy-start(s32[1,1,128]{2,1,0:T(1,128)} %param.11) | copy-start | bytes 1540
  4.4 25.0 %copy-start.6 = (s32[1,1,128]{2,1,0:T(1,128)S(1)}, s32[1,1,128]{2,1,0:T(1,128)}, u32[]{:S(2)}) copy-start(s32[1,1,128]{2,1,0:T(1,128)} %param.13) | copy-start | bytes 1540
